TPU v7x, 32 devices: a whole 2x2x4 slice. The times are simulated.
32 devices in a mesh: dp: 8 (over z, x), shard: 4 (over y, core).
Axes of the slice: x: 2, y: 2, z: 4, core: 2. Of those that a mesh axis runs over, the one named last changes fastest.
Arguments:
- images: bfloat16 [8, 591, 768], P('dp'), may hold values from -6 to 6
- out_grad: bfloat16 [8, 591, 768], P('dp'), may hold values from -6 to 6
- slot_kind: int32 [8], P('dp'), may hold values from 0 to 1
- small_index: int32 [197, 197], replicated, may hold values from 0 to 731, as said below
- large_index: int32 [577, 577], replicated, may hold values from 0 to 2211, as said below
- qkv_weight: bfloat16 [768, 3, 768], P('dp', None, 'shard'), may hold values from -0.21875 to 0.21875
- out_weight: bfloat16 [768, 768], P('shard', 'dp'), may hold values from -1.75 to 1.75
- fc1_weight: bfloat16 [768, 3072], P('dp', 'shard'), may hold values from -0.21875 to 0.21875
- fc2_weight: bfloat16 [3072, 768], P('shard', 'dp'), may hold values from -0.109375 to 0.109375
- norm1_gain: bfloat16 [768], P('dp'), may hold values from 0.099609375 to 1.8984375
- norm1_shift: bfloat16 [768], P('dp'), may hold values from -1.796875 to 1.796875
- query_bias: bfloat16 [768], P('shard'), may hold values from -1.796875 to 1.796875
- value_bias: bfloat16 [768], P('shard'), may hold values from -1.796875 to 1.796875
- out_bias: bfloat16 [768], P('dp'), may hold values from -1.796875 to 1.796875
- gamma_attn: bfloat16 [768], P('dp'), may hold values from 0.099609375 to 1.8984375
- norm2_gain: bfloat16 [768], P('dp'), may hold values from 0.099609375 to 1.8984375
- norm2_shift: bfloat16 [768], P('dp'), may hold values from -1.796875 to 1.796875
- fc1_bias: bfloat16 [3072], P('shard'), may hold values from -1.796875 to 1.796875
- fc2_bias: bfloat16 [768], P('dp'), may hold values from -1.796875 to 1.796875
- gamma_mlp: bfloat16 [768], P('dp'), may hold values from 0.099609375 to 1.8984375
- small_table: bfloat16 [732, 12], P(None, 'shard'), may hold values from -4 to 4
- large_table: bfloat16 [2212, 12], P(None, 'shard'), may hold values from -4 to 4
Outputs:
- layer_out: bfloat16 [8, 591, 768], P('dp')
- input_grad: bfloat16 [8, 591, 768], P('dp')
- qkv_weight_grad: float32 [768, 3, 768], P('dp', None, 'shard')
- out_weight_grad: float32 [768, 768], P('shard', 'dp')
- fc1_weight_grad: float32 [768, 3072], P('dp', 'shard')
- fc2_weight_grad: float32 [3072, 768], P('shard', 'dp')
- norm1_gain_grad: float32 [768], P('dp')
- norm1_shift_grad: float32 [768], P('dp')
- query_bias_grad: float32 [768], P('shard')
- value_bias_grad: float32 [768], P('shard')
- out_bias_grad: float32 [768], P('dp')
- gamma_attn_grad: float32 [768], P('dp')
- norm2_gain_grad: float32 [768], P('dp')
- norm2_shift_grad: float32 [768], P('dp')
- fc1_bias_grad: float32 [3072], P('shard')
- fc2_bias_grad: float32 [768], P('dp')
- gamma_mlp_grad: float32 [768], P('dp')
- small_table_grad: float32 [732, 12], P(None, 'shard')
- large_table_grad: float32 [2212, 12], P(None, 'shard')
Inputs may be any that keep to these rules, and one draw needn't show every extreme that they name: `slot_kind`: 0: three images of 197 rows; 1: one image of 577 rows. `small_index`: every entry of the table is named by some pair. `large_index`: every entry of the table is named by some pair.
All inputs are finite; a program needn't handle non-finite values.
Results may differ from a plain program's by a relative error of at most 0.012.
The roundings to bfloat16 on the way count: a program that leaves them out, or rounds other values in their place, can miss the bound.
Values may be sent and summed in bfloat16 or wider, within the bound.
A program may use at most 384 MiB of HBM per device.

v0:
```python
import jax
import jax.numpy as jnp
from jax import lax
from jax.sharding import PartitionSpec as P

HEAD_DIM = 64
SMALL_LEN = 197
LARGE_LEN = 577


EPS = 1e-06


def split_up(value, dim, peers):
    lengths = value.shape
    parts = value.reshape(*lengths[:dim], peers, lengths[dim] // peers, *lengths[dim + 1 :])
    return jnp.moveaxis(parts, dim, 0)


def sent_and_summed(value, axis, dim):
    parts = split_up(value, dim, lax.axis_size(axis))
    arrived = lax.all_to_all(parts, axis, split_axis=0, concat_axis=0, tiled=True)
    return arrived.astype(jnp.float32).sum(axis=0)


def layer_norm(activations, norm_gain, norm_shift):
    center = activations - jnp.mean(activations, -1, keepdims=True)
    inverse = lax.rsqrt(jnp.mean(center * center, -1, keepdims=True) + EPS)
    normal = center * inverse
    return (normal * norm_gain + norm_shift, normal, inverse)


def norm_back(grad_normed, normal, inverse, norm_gain):
    scaled = grad_normed * norm_gain
    return inverse * (
        scaled
        - jnp.mean(scaled, -1, keepdims=True)
        - normal * jnp.mean(scaled * normal, -1, keepdims=True)
    )


def gelu_slope(hidden):
    cumulative = 0.5 * (1.0 + jax.scipy.special.erf(hidden * 0.7071067811865476))
    return cumulative + hidden * jnp.exp(-0.5 * hidden * hidden) * 0.3989422804014327


def head_view(tensor):
    return tensor.reshape(tensor.shape[0], tensor.shape[1], -1, HEAD_DIM)


def table_product(grad_scores, index_map, table_size):
    head_count = grad_scores.shape[1]
    flat_grads = (
        jnp.transpose(grad_scores, (1, 0, 2, 3)).reshape(head_count, -1).astype(jnp.float32)
    )
    flat_index = jnp.tile(index_map.reshape(-1), grad_scores.shape[0])

    def one_head(head_grads):
        return jax.ops.segment_sum(head_grads, flat_index, num_segments=table_size)

    return jax.vmap(one_head)(flat_grads)


def score_weights(query_rows, key_rows, pair_bias):
    scores = jnp.einsum(
        "nlhd,nmhd->nhlm",
        head_view(query_rows),
        head_view(key_rows),
        preferred_element_type=jnp.float32,
    )
    return jax.nn.softmax(scores * HEAD_DIM ** (-0.5) + pair_bias[None], axis=-1)


def attend_forward(query_rows, key_rows, value_rows, pair_bias):
    softmax_weights = score_weights(query_rows, key_rows, pair_bias).astype(jnp.bfloat16)
    combined = jnp.einsum(
        "nhlm,nmhd->nlhd",
        softmax_weights,
        head_view(value_rows),
        preferred_element_type=jnp.float32,
    )
    return combined.reshape(query_rows.shape).astype(jnp.bfloat16)


def attend_backward(query_rows, key_rows, value_rows, pair_bias, grad_combined):
    softmax_weights = score_weights(query_rows, key_rows, pair_bias)
    grad_heads = head_view(grad_combined)
    grad_weights = jnp.einsum(
        "nlhd,nmhd->nhlm", grad_heads, head_view(value_rows), preferred_element_type=jnp.float32
    )
    grad_scores = (
        softmax_weights
        * (grad_weights - jnp.sum(softmax_weights * grad_weights, -1, keepdims=True))
    ).astype(jnp.bfloat16)
    factor = HEAD_DIM ** (-0.5)
    layout = query_rows.shape
    grad_queries = (
        jnp.einsum(
            "nhlm,nmhd->nlhd", grad_scores, head_view(key_rows), preferred_element_type=jnp.float32
        )
        * factor
    )
    grad_keys = (
        jnp.einsum(
            "nhlm,nlhd->nmhd",
            grad_scores,
            head_view(query_rows),
            preferred_element_type=jnp.float32,
        )
        * factor
    )
    grad_values = jnp.einsum(
        "nhlm,nlhd->nmhd",
        softmax_weights.astype(jnp.bfloat16),
        grad_heads,
        preferred_element_type=jnp.float32,
    )
    return (
        grad_queries.reshape(layout).astype(jnp.bfloat16),
        grad_keys.reshape(layout).astype(jnp.bfloat16),
        grad_values.reshape(layout).astype(jnp.bfloat16),
        grad_scores,
    )


def heads_forward(operands, table_rows, index_map, images_count, length):
    total_rows = operands[0].shape[0]
    used_rows = images_count * length
    pair_bias = jnp.take(table_rows, index_map, axis=1)
    shaped = [member[:used_rows].reshape(images_count, length, -1) for member in operands]
    combined = attend_forward(shaped[0], shaped[1], shaped[2], pair_bias)
    return jnp.pad(combined.reshape(used_rows, -1), ((0, total_rows - used_rows), (0, 0)))


def heads_backward(operands, grad_rows, table_rows, index_map, images_count, length):
    total_rows = operands[0].shape[0]
    used_rows = images_count * length
    pair_bias = jnp.take(table_rows, index_map, axis=1)
    shaped = [member[:used_rows].reshape(images_count, length, -1) for member in operands]
    grad_shaped = grad_rows[:used_rows].reshape(images_count, length, -1)
    block_grads = attend_backward(shaped[0], shaped[1], shaped[2], pair_bias, grad_shaped)
    padding = ((0, total_rows - used_rows), (0, 0))
    row_grads = tuple(
        (jnp.pad(block_grads[position].reshape(used_rows, -1), padding) for position in range(3))
    )
    return (row_grads, table_product(block_grads[3], index_map, table_rows.shape[1]))


def slot_forward(kind_value, operands, small_rows, large_rows, small_index, large_index):

    def small_case(members):
        return heads_forward(members, small_rows, small_index, 3, SMALL_LEN)

    def large_case(members):
        return heads_forward(members, large_rows, large_index, 1, LARGE_LEN)

    return lax.cond(kind_value == 1, large_case, small_case, operands)


def slot_backward(
    kind_value, operands, grad_rows, small_rows, large_rows, small_index, large_index
):

    def small_case(members):
        row_grads, table_grad = heads_backward(
            members[:3], members[3], small_rows, small_index, 3, SMALL_LEN
        )
        return (row_grads, table_grad, jnp.zeros_like(large_rows))

    def large_case(members):
        row_grads, table_grad = heads_backward(
            members[:3], members[3], large_rows, large_index, 1, LARGE_LEN
        )
        return (row_grads, jnp.zeros_like(small_rows), table_grad)

    return lax.cond(kind_value == 1, large_case, small_case, operands + (grad_rows,))


def split_parameters(gathered):
    qkv_matrix = gathered[0].reshape(gathered[0].shape[0], -1)
    matrices = (qkv_matrix, gathered[1], gathered[2], gathered[3])
    vectors = tuple((member.astype(jnp.float32) for member in gathered[4:]))
    return (matrices, vectors)


def attention_inputs(inputs, qkv_matrix, vectors, query_shift, value_shift):
    local_width = query_shift.shape[0]
    normed, normal, inverse = layer_norm(inputs, vectors[0], vectors[1])
    normed = normed.astype(jnp.bfloat16)
    projected = jnp.dot(normed, qkv_matrix, preferred_element_type=jnp.float32)
    query_rows = (projected[:, :local_width] + query_shift).astype(jnp.bfloat16)
    key_rows = projected[:, local_width : 2 * local_width].astype(jnp.bfloat16)
    value_rows = (projected[:, 2 * local_width :] + value_shift).astype(jnp.bfloat16)
    return (normed, normal, inverse, query_rows, key_rows, value_rows)


def on_device(
    images,
    out_grad,
    slot_kind,
    small_index,
    large_index,
    qkv_weight,
    out_weight,
    fc1_weight,
    fc2_weight,
    norm1_gain,
    norm1_shift,
    query_bias,
    value_bias,
    out_bias,
    gamma_attn,
    norm2_gain,
    norm2_shift,
    fc1_bias,
    fc2_bias,
    gamma_mlp,
    small_table,
    large_table,
):
    gathered = (
        lax.all_gather(qkv_weight, "dp", axis=0, tiled=True),
        lax.all_gather(fc1_weight, "dp", axis=0, tiled=True),
        lax.all_gather(out_weight, "dp", axis=1, tiled=True),
        lax.all_gather(fc2_weight, "dp", axis=1, tiled=True),
        lax.all_gather(norm1_gain, "dp", axis=0, tiled=True),
        lax.all_gather(norm1_shift, "dp", axis=0, tiled=True),
        lax.all_gather(out_bias, "dp", axis=0, tiled=True),
        lax.all_gather(gamma_attn, "dp", axis=0, tiled=True),
        lax.all_gather(norm2_gain, "dp", axis=0, tiled=True),
        lax.all_gather(norm2_shift, "dp", axis=0, tiled=True),
        lax.all_gather(fc2_bias, "dp", axis=0, tiled=True),
        lax.all_gather(gamma_mlp, "dp", axis=0, tiled=True),
    )
    matrices, vectors = split_parameters(
        (gathered[0], gathered[1], gathered[2], gathered[3]) + tuple(gathered[4:])
    )
    query_shift = query_bias.astype(jnp.float32)
    value_shift = value_bias.astype(jnp.float32)
    hidden_shift = fc1_bias.astype(jnp.float32)
    small_rows = small_table.astype(jnp.float32).T
    large_rows = large_table.astype(jnp.float32).T
    slots_here, slot_rows, model_width = images.shape
    positions = jnp.arange(slot_rows)
    live_rows = jnp.where(slot_kind[:, None] == 1, positions[None, :] < LARGE_LEN, True)
    live_rows = live_rows.astype(jnp.float32).reshape(-1, 1)
    inputs = images.reshape(-1, model_width).astype(jnp.float32)
    normed_one, normal_one, inverse_one, query_rows, key_rows, value_rows = attention_inputs(
        inputs, matrices[0], vectors, query_shift, value_shift
    )
    slot_index = 0
    pieces = slot_forward(
        slot_kind[slot_index],
        (query_rows, key_rows, value_rows),
        small_rows,
        large_rows,
        small_index,
        large_index,
    )
    branch_part = jnp.dot(pieces, matrices[2], preferred_element_type=jnp.float32)
    branch = lax.psum(branch_part, "shard") + vectors[2]
    middle = inputs + vectors[3] * branch
    normed_two, normal_two, inverse_two = layer_norm(middle, vectors[4], vectors[5])
    normed_two = normed_two.astype(jnp.bfloat16)
    hidden = jnp.dot(normed_two, matrices[1], preferred_element_type=jnp.float32) + hidden_shift
    active = jax.nn.gelu(hidden, approximate=False).astype(jnp.bfloat16)
    result_part = jnp.dot(active, matrices[3], preferred_element_type=jnp.float32)
    result = lax.psum(result_part.astype(jnp.bfloat16), "shard").astype(jnp.float32) + vectors[6]
    layer_out = (
        ((middle + vectors[7] * result) * live_rows).astype(jnp.bfloat16).reshape(images.shape)
    )
    regathered = (
        lax.all_gather(qkv_weight, "dp", axis=0, tiled=True),
        lax.all_gather(fc1_weight, "dp", axis=0, tiled=True),
        lax.all_gather(out_weight, "dp", axis=1, tiled=True),
        lax.all_gather(fc2_weight, "dp", axis=1, tiled=True),
        lax.all_gather(norm1_gain, "dp", axis=0, tiled=True),
        lax.all_gather(norm1_shift, "dp", axis=0, tiled=True),
        lax.all_gather(out_bias, "dp", axis=0, tiled=True),
        lax.all_gather(gamma_attn, "dp", axis=0, tiled=True),
        lax.all_gather(norm2_gain, "dp", axis=0, tiled=True),
        lax.all_gather(norm2_shift, "dp", axis=0, tiled=True),
        lax.all_gather(fc2_bias, "dp", axis=0, tiled=True),
        lax.all_gather(gamma_mlp, "dp", axis=0, tiled=True),
    )
    matrices, vectors = split_parameters(tuple(regathered))
    grad_out = out_grad.reshape(-1, model_width).astype(jnp.float32) * live_rows
    grad_gamma_mlp = jnp.sum(grad_out * result, 0)
    grad_result = (grad_out * vectors[7]).astype(jnp.bfloat16)
    grad_fc2_bias = jnp.sum(grad_result.astype(jnp.float32), 0)
    grad_fc2_weight = jnp.einsum(
        "rf,rd->fd", active, grad_result, preferred_element_type=jnp.float32
    )
    grad_active = jnp.einsum(
        "rd,fd->rf", grad_result, matrices[3], preferred_element_type=jnp.float32
    )
    grad_hidden = (grad_active * gelu_slope(hidden)).astype(jnp.bfloat16)
    grad_fc1_bias = jnp.sum(grad_hidden.astype(jnp.float32), 0)
    grad_fc1_weight = jnp.einsum(
        "rd,rf->df", normed_two, grad_hidden, preferred_element_type=jnp.float32
    )
    grad_normed_part = jnp.einsum(
        "rf,df->rd", grad_hidden, matrices[1], preferred_element_type=jnp.float32
    )
    grad_normed_two = lax.psum(grad_normed_part, "shard")
    grad_norm2_gain = jnp.sum(grad_normed_two * normal_two, 0)
    grad_norm2_shift = jnp.sum(grad_normed_two, 0)
    grad_middle = grad_out + norm_back(grad_normed_two, normal_two, inverse_two, vectors[4])
    grad_gamma_attn = jnp.sum(grad_middle * branch, 0)
    grad_branch = (grad_middle * vectors[3]).astype(jnp.bfloat16)
    grad_out_bias = jnp.sum(grad_branch.astype(jnp.float32), 0)
    grad_out_weight = jnp.einsum(
        "rd,re->de", pieces, grad_branch, preferred_element_type=jnp.float32
    )
    grad_attended = jnp.einsum(
        "re,de->rd", grad_branch, matrices[2], preferred_element_type=jnp.float32
    ).astype(jnp.bfloat16)
    normed_one, normal_one, inverse_one, query_rows, key_rows, value_rows = attention_inputs(
        inputs, matrices[0], vectors, query_shift, value_shift
    )
    grad_parts = ([], [], [])
    slot_index = 0
    row_grads, small_piece, large_piece = slot_backward(
        slot_kind[slot_index],
        (query_rows, key_rows, value_rows),
        grad_attended,
        small_rows,
        large_rows,
        small_index,
        large_index,
    )
    for position in range(3):
        grad_parts[position].append(row_grads[position])
    grad_queries = jnp.concatenate(grad_parts[0], 0)
    grad_keys = jnp.concatenate(grad_parts[1], 0)
    grad_values = jnp.concatenate(grad_parts[2], 0)
    grad_projected = jnp.concatenate((grad_queries, grad_keys, grad_values), 1)
    grad_qkv_weight = jnp.einsum(
        "rd,re->de", normed_one, grad_projected, preferred_element_type=jnp.float32
    )
    grad_qkv_weight = grad_qkv_weight.reshape(model_width, 3, -1)
    grad_query_bias = jnp.sum(grad_queries.astype(jnp.float32), 0)
    grad_value_bias = jnp.sum(grad_values.astype(jnp.float32), 0)
    grad_first_part = jnp.einsum(
        "re,de->rd", grad_projected, matrices[0], preferred_element_type=jnp.float32
    )
    grad_normed_one = lax.psum(grad_first_part, "shard")
    grad_norm1_gain = jnp.sum(grad_normed_one * normal_one, 0)
    grad_norm1_shift = jnp.sum(grad_normed_one, 0)
    input_grad = grad_middle + norm_back(grad_normed_one, normal_one, inverse_one, vectors[0])
    input_grad = input_grad.astype(jnp.bfloat16).reshape(images.shape)
    local_sums = lax.psum(
        (small_piece.T, large_piece.T, grad_query_bias, grad_value_bias, grad_fc1_bias), "dp"
    )
    ordered = (
        sent_and_summed(grad_qkv_weight.astype(jnp.bfloat16), "dp", 0),
        sent_and_summed(grad_out_weight.astype(jnp.bfloat16), "dp", 1),
        sent_and_summed(grad_fc1_weight.astype(jnp.bfloat16), "dp", 0),
        sent_and_summed(grad_fc2_weight.astype(jnp.bfloat16), "dp", 1),
        sent_and_summed(grad_norm1_gain.astype(jnp.bfloat16), "dp", 0),
        sent_and_summed(grad_norm1_shift.astype(jnp.bfloat16), "dp", 0),
        sent_and_summed(grad_out_bias.astype(jnp.bfloat16), "dp", 0),
        sent_and_summed(grad_gamma_attn.astype(jnp.bfloat16), "dp", 0),
        sent_and_summed(grad_norm2_gain.astype(jnp.bfloat16), "dp", 0),
        sent_and_summed(grad_norm2_shift.astype(jnp.bfloat16), "dp", 0),
        sent_and_summed(grad_fc2_bias.astype(jnp.bfloat16), "dp", 0),
        sent_and_summed(grad_gamma_mlp.astype(jnp.bfloat16), "dp", 0),
    )
    return (
        layer_out,
        input_grad,
        ordered[0],
        ordered[1],
        ordered[2],
        ordered[3],
        ordered[4],
        ordered[5],
        local_sums[2],
        local_sums[3],
        ordered[6],
        ordered[7],
        ordered[8],
        ordered[9],
        local_sums[4],
        ordered[10],
        ordered[11],
        local_sums[0],
        local_sums[1],
    )


def solution(mesh):
    return jax.shard_map(
        on_device,
        mesh=mesh,
        in_specs=(
            P("dp", None, None),
            P("dp", None, None),
            P("dp"),
            P(),
            P(),
            P("dp", None, "shard"),
            P("shard", "dp"),
            P("dp", "shard"),
            P("shard", "dp"),
            P("dp"),
            P("dp"),
            P("shard"),
            P("shard"),
            P("dp"),
            P("dp"),
            P("dp"),
            P("dp"),
            P("shard"),
            P("dp"),
            P("dp"),
            P(None, "shard"),
            P(None, "shard"),
        ),
        out_specs=(
            P("dp", None, None),
            P("dp", None, None),
            P("dp", None, "shard"),
            P("shard", "dp"),
            P("dp", "shard"),
            P("shard", "dp"),
            P("dp"),
            P("dp"),
            P("shard"),
            P("shard"),
            P("dp"),
            P("dp"),
            P("dp"),
            P("dp"),
            P("shard"),
            P("dp"),
            P("dp"),
            P(None, "shard"),
            P(None, "shard"),
        ),
        check_vma=False,
    )
```

profile of v0, /device:TPU:0, one launch (start us, length us, event | category | flops | bytes accessed | tf_op | source)
XLA Modules:
  0.0 3929.6 jit_solution(2024037691738949575)
XLA Ops:
  18.7 39.5 %all-reduce.13 = (bf16[768]{0:T(1024)(128)(2,1)S(1)}, bf16[768]{0:T(1024)(128)(2,1)S(1)}, bf16[768]{0:T(1024)(128)(2,1)}, bf16[768]{0:T(1024)(128)(2,1)}, bf16[7...) all-reduce(bf16[768]{0:T(1024)(128)(2,1)S(1)} %dynamic-update-slice, ...), channel_id=1, replica_groups=mesh['dp'=8,'shard'=4] {'dp'}, use_global_device_ids=true, to_apply=%add.6 | all-reduce | flops 6144 | bytes 24576
  61.5 33.3 all_gather.49
  95.3 37.9 all_gather.48
  133.2 3.4 copy.156
  136.7 2.2 fusion.102
  140.4 177.3 %conditional.2 = (bf16[591,192]{0,1:T(8,128)(2,1)}) conditional(s32[]{:T(128)} %convert_element_type.428, (bf16[591,192]{0,1:T(8,128)(2,1)S(1)}, bf16[591,192]{0,1:T(8,128)(2,1)S(1)}, f32[3,732]{0,1:T(8,128)S(1)}, s32[197,197]{1,0:T(8,128)S(1)}, bf16[591,192]{0,1:T(8,128)(2,1)}) %tuple.79, (bf16[591,192]{0,1:T(8,128)(2,1)S(1)}, ...), branch_computations={%region_2.6_spmd, %region_5.10_spmd} | conditional | flops 267123616 | bytes 77260064 | solution.py:157
  150.2 140.9 %gather_fusion = f32[38809,3]{1,0:T(8,128)} fusion(f32[3,732]{0,1:T(8,128)S(1)} %get-tuple-element.45, s32[38912]{0:T(1024)} %pad_clamp_fusion), kind=kCustom, calls=%fused_computation.clone | custom fusion | bytes 1086652 | tf_op jit(solution)/shard_map/cond/branch_0_fun/jit(_take)/gather | solution.py:129
  291.2 11.4 copy.120
  302.6 2.6 reshape.609
  305.2 2.0 select_bitcast_fusion
  307.1 2.1 copy.121
  309.3 3.3 fusion.118
  317.7 2.8 fusion.126
  321.7 14.9 all-reduce.23.cloned.1.call-start
  336.8 644.6 %all-reduce.19.cloned.1.call-done = f32[591,768]{1,0:T(8,128)} async-done(((f32[591,768]{1,0:T(8,128)}), f32[591,768]{1,0:T(8,128)}) %all-reduce.19.cloned.1.call-update) | async-done | bytes 1815568 | tf_op jit(solution)/shard_map/psum | solution.py:261
  981.4 2.1 fusion.116
  985.2 7.3 fusion.80
  992.5 27.8 all-gather.5.cloned.1.call-done
  1020.3 4.2 convert_reduce_fusion.4
  1025.4 2.2 fusion.127
  1027.7 3.4 convolution_convert_fusion.4
  1031.1 42.2 %all-reduce.23.cloned.1.call-done = f32[591,768]{1,0:T(8,128)} async-done(((f32[591,768]{1,0:T(8,128)}), f32[591,768]{1,0:T(8,128)}) %all-reduce.23.cloned.1.call-update) | async-done | bytes 1815568 | tf_op jit(solution)/shard_map/psum | solution.py:305
  1073.3 3.4 multiply_reduce_fusion.2
  1076.7 34.7 all-reduce.21.cloned.1.call-done
  1111.5 5.2 multiply_reduce_fusion.3
  1119.1 828.0 %conditional.3 = (bf16[591,192]{0,1:T(8,128)(2,1)S(1)}, bf16[591,192]{0,1:T(8,128)(2,1)S(1)}, bf16[591,192]{0,1:T(8,128)(2,1)S(1)}, f32[3,732]{0,1:T(8,128)S(1)}, f32[3,2212]{1,0:T(4,128)S(1)}) conditional(s32[]{:T(128)} %convert_element_type.428, (bf16[591,192]{0,1:T(8,128)(2,1)S(1)}, bf16[591,192]{0,1:T(8,128)(2,1)S(1)}, ...), branch_computations={%region_15.22_spmd, %region_20.27_spmd} | conditional | flops 659089536 | bytes 147295008 | solution.py:176
  1127.0 128.5 %gather_fusion.1 = f32[38809,3]{1,0:T(8,128)} fusion(f32[3,732]{0,1:T(8,128)S(1)} %get-tuple-element.61, s32[38912]{0:T(1024)S(1)} %pad_clamp_fusion.2), kind=kCustom, calls=%fused_computation.2.clone | custom fusion | bytes 1086652 | tf_op jit(solution)/shard_map/cond/branch_0_fun/jit(_take)/gather | solution.py:138
  1255.5 11.1 copy.131
  1276.8 3.3 reshape.541
  1281.1 27.8 copy.145
  1308.9 620.6 %scatter_custom_fusion = f32[3,732]{0,1:T(8,128)S(1)} fusion(s32[116427]{0:T(1024)} %reshape.542, f32[116427,3]{1,0:T(8,128)} %copy.145, f32[]{:T(128)} %constant.21.clone), kind=kCustom, calls=%fused_computation.67 | custom fusion | flops 349281 | bytes 9296 | tf_op jit(solution)/shard_map/cond/branch_0_fun/vmap()/scatter-add | solution.py:59
  1948.8 3.4 fusion.128
  1953.3 1773.5 %all-to-all-start.10 = ((bf16[8,1,96]{2,1,0:T(2,128)(2,1)}), bf16[8,1,96]{2,1,0:T(2,128)(2,1)S(1)}, u32[]{:S(2)}, u32[]{:S(2)}) async-start(bf16[8,1,96]{2,1,0:T(2,128)(2,1)} %all_to_all.63), calls=%async_computation.10 | async-start | bytes 8192 | tf_op jit(solution)/shard_map/all_to_all | solution.py:22
  3727.5 5.7 all-to-all-done.10
  3733.2 3.3 all-to-all-start.11
  3737.2 5.6 all-to-all-done.11
  3742.8 3.3 all-to-all-start.7
  3746.8 5.6 all-to-all-done.7
  3752.5 3.3 all-to-all-start.9
  3756.5 5.6 all-to-all-done.9
  3762.1 3.3 all-to-all-start.8
  3766.1 5.6 all-to-all-done.8
  3771.8 3.3 all-to-all-start.6
  3778.5 2.9 all-to-all-done.6
  3781.4 3.5 all-to-all-start.1
  3784.9 2.4 fusion.72
  3788.0 6.0 all-to-all-done.1
  3794.0 3.3 all-to-all-start.5
  3798.0 5.7 all-to-all-done.5
  3803.8 3.3 all-to-all-start.4
  3807.1 3.5 convolution_convert_fusion.2
  3810.6 3.3 all-to-all-done.4
  3813.9 4.2 all-to-all-start.3
  3818.2 3.6 convolution_convert_fusion.3
  3821.8 23.6 all-to-all-done.3
  3845.4 4.3 all-to-all-start.2
  3850.4 2.0 convolution_convert_fusion.5
  3852.4 2.4 reshape.501
  3856.3 39.3 all-reduce.12
  3897.7 4.3 all-to-all-start
  3904.2 3.0 fusion.100
  3908.4 2.2 convert_reduce_fusion.1
  3910.5 2.2 convert_reduce_fusion.2
  3912.7 7.1 all-to-all-done
  (269 shorter events, 75.2 us)
Async XLA Ops:
  8.0 53.2 %copy-start.42 = (bf16[192,96]{1,0:T(8,128)(2,1)S(1)}, bf16[192,96]{1,0:T(8,128)(2,1)}, u32[]{:S(2)}) copy-start(bf16[192,96]{1,0:T(8,128)(2,1)} %param.36) | copy-start | bytes 110596
  8.0 53.3 %copy-start.35 = (bf16[96,3,192]{2,0,1:T(8,128)(2,1)S(1)}, bf16[96,3,192]{2,0,1:T(8,128)(2,1)}, u32[]{:S(2)}) copy-start(bf16[96,3,192]{2,0,1:T(8,128)(2,1)} %param.35) | copy-start | bytes 331780
  8.0 86.8 %copy-start.61 = (bf16[732,3]{0,1:T(4,128)(2,1)S(1)}, bf16[732,3]{0,1:T(4,128)(2,1)}, u32[]{:S(2)}) copy-start(bf16[732,3]{0,1:T(4,128)(2,1)} %param.50) | copy-start | bytes 13180
  8.1 86.9 %copy-start.55 = (bf16[2212,3]{0,1:T(4,128)(2,1)S(1)}, bf16[2212,3]{0,1:T(4,128)(2,1)}, u32[]{:S(2)}) copy-start(bf16[2212,3]{0,1:T(4,128)(2,1)} %param.51) | copy-start | bytes 39820
  8.1 973.3 %all-reduce.19.cloned.1.call-start = ((), (), s32[]{:S(2)}) async-start(), calls=%async_computation.12 | async-start | bytes 3637248 | tf_op jit(solution)/shard_map/psum | solution.py:261
  58.2 78.4 %copy-start.63 = (f32[768]{0:T(1024)}, f32[768]{0:T(1024)S(1)}, u32[]{:S(2)}) copy-start(f32[768]{0:T(1024)S(1)} %convert_element_type.430) | copy-start | bytes 9220
  58.2 78.4 %copy-start.51 = (f32[768]{0:T(1024)}, f32[768]{0:T(1024)S(1)}, u32[]{:S(2)}) copy-start(f32[768]{0:T(1024)S(1)} %convert_element_type.429) | copy-start | bytes 9220
  59.6 77.0 %copy-start.40 = (f32[591]{0:T(1024)}, f32[591]{0:T(1024)S(1)}, u32[]{:S(2)}) copy-start(f32[591]{0:T(1024)S(1)} %broadcast_multiply_fusion.5) | copy-start | bytes 7096
  61.2 75.4 %copy-start.53 = (f32[591]{0:T(1024)}, f32[591]{0:T(1024)S(1)}, u32[]{:S(2)}) copy-start(f32[591]{0:T(1024)S(1)} %add_rsqrt_fusion.1) | copy-start | bytes 7096
  95.3 41.4 %copy-start.3 = (bf16[1,591,768]{2,1,0:T(8,128)(2,1)S(1)}, bf16[1,591,768]{2,1,0:T(8,128)(2,1)}, u32[]{:S(2)}) copy-start(bf16[1,591,768]{2,1,0:T(8,128)(2,1)} %param.30) | copy-start | bytes 2723332
  317.7 19.0 copy-start.72
  317.7 19.0 copy-start.71
  317.7 19.0 copy-start.70
  317.7 19.1 copy-start.69
  317.7 19.1 copy-start.68
  317.7 19.1 copy-start.67
  320.6 664.6 %all-gather.3.cloned.1.call-start = ((), (), s32[]{:S(2)}) async-start(), calls=%async_computation.13 | async-start | bytes 1327104 | tf_op jit(solution)/shard_map/all_gather | solution.py:223
  321.2 699.1 %all-gather.5.cloned.1.call-start = ((), (), s32[]{:S(2)}) async-start(), calls=%async_computation.14 | async-start | bytes 1327104 | tf_op jit(solution)/shard_map/all_gather | solution.py:225
  321.7 751.5 %all-reduce.23.cloned.1.call-start = ((), (), s32[]{:S(2)}) async-start(), calls=%async_computation.16 | async-start | bytes 3637248 | tf_op jit(solution)/shard_map/psum | solution.py:305
  336.6 774.8 %copy-start.45 = (f32[591]{0:T(1024)}, f32[591]{0:T(1024)S(1)}, u32[]{:S(2)}) copy-start(f32[591]{0:T(1024)S(1)} %fusion.107) | copy-start | bytes 7096
  336.7 774.8 %copy-start.43 = (f32[768]{0:T(1024)}, f32[768]{0:T(1024)S(1)}, u32[]{:S(2)}) copy-start(f32[768]{0:T(1024)S(1)} %convert_element_type.439) | copy-start | bytes 9220
  336.7 774.7 %copy-start.47 = (f32[768]{0:T(1024)}, f32[768]{0:T(1024)S(1)}, u32[]{:S(2)}) copy-start(f32[768]{0:T(1024)S(1)} %convert_element_type.438) | copy-start | bytes 9220
  336.8 648.4 %copy-start.65 = (f32[768]{0:T(1024)}, f32[768]{0:T(1024)S(1)}, u32[]{:S(2)}) copy-start(f32[768]{0:T(1024)S(1)} %convert_element_type.440) | copy-start | bytes 9220
  983.5 127.9 %copy-start.38 = (f32[591]{0:T(1024)}, f32[591]{0:T(1024)S(1)}, u32[]{:S(2)}) copy-start(f32[591]{0:T(1024)S(1)} %broadcast_multiply_fusion.4) | copy-start | bytes 7096
  985.1 126.4 %copy-start.49 = (f32[591]{0:T(1024)}, f32[591]{0:T(1024)S(1)}, u32[]{:S(2)}) copy-start(f32[591]{0:T(1024)S(1)} %add_rsqrt_fusion) | copy-start | bytes 7096
  1020.3 5.1 copy-start.73
  1027.6 83.8 %all-reduce.21.cloned.1.call-start = ((), (), s32[]{:S(2)}) async-start(), calls=%async_computation.15 | async-start | bytes 1818624 | tf_op jit(solution)/shard_map/psum | solution.py:268
  1031.1 2753.8 %all-reduce.25.cloned.1.call-start = ((), (), s32[]{:S(2)}) async-start(), calls=%async_computation.17 | async-start | bytes 3637248 | tf_op jit(solution)/shard_map/psum | solution.py:347
  1119.1 4.6 copy-start.29
  1119.1 5.6 copy-start.20
  1123.7 143.9 %copy-start.18 = (bf16[3,197,3,64]{1,0,3,2:T(4,128)(2,1)}, bf16[3,197,3,64]{1,0,3,2:T(4,128)(2,1)S(1)}, u32[]{:S(2)}) copy-start(bf16[3,197,3,64]{1,0,3,2:T(4,128)(2,1)S(1)} %reshape.483) | copy-start | bytes 680836 | tf_op jit(solution)/shard_map/cond
  1952.2 1774.6 %copy-start.60 = (bf16[768]{0:T(1024)(128)(2,1)S(1)}, bf16[768]{0:T(1024)(128)(2,1)}, u32[]{:S(2)}) copy-start(bf16[768]{0:T(1024)(128)(2,1)} %get-tuple-element.194) | copy-start | bytes 4612
  1952.2 1784.3 %copy-start.59 = (bf16[768]{0:T(1024)(128)(2,1)S(1)}, bf16[768]{0:T(1024)(128)(2,1)}, u32[]{:S(2)}) copy-start(bf16[768]{0:T(1024)(128)(2,1)} %get-tuple-element.177) | copy-start | bytes 4612
  1952.2 1794.0 %copy-start.57 = (bf16[768]{0:T(1024)(128)(2,1)S(1)}, bf16[768]{0:T(1024)(128)(2,1)}, u32[]{:S(2)}) copy-start(bf16[768]{0:T(1024)(128)(2,1)} %get-tuple-element.162) | copy-start | bytes 4612
  1952.2 1803.6 %copy-start.56 = (bf16[768]{0:T(1024)(128)(2,1)S(1)}, bf16[768]{0:T(1024)(128)(2,1)}, u32[]{:S(2)}) copy-start(bf16[768]{0:T(1024)(128)(2,1)} %get-tuple-element.156) | copy-start | bytes 4612
  1952.2 1813.3 %copy-start.58 = (bf16[768]{0:T(1024)(128)(2,1)S(1)}, bf16[768]{0:T(1024)(128)(2,1)}, u32[]{:S(2)}) copy-start(bf16[768]{0:T(1024)(128)(2,1)} %get-tuple-element.179) | copy-start | bytes 4612
  1952.2 1822.9 %copy-start.10 = (bf16[591,768]{1,0:T(8,128)(2,1)S(1)}, bf16[591,768]{1,0:T(8,128)(2,1)}, u32[]{:S(2)}) copy-start(bf16[591,768]{1,0:T(8,128)(2,1)} %copy-done.9) | copy-start | bytes 2723332
  1952.2 1822.9 %copy-start.23 = (bf16[591,192]{0,1:T(8,128)(2,1)S(1)}, bf16[591,192]{0,1:T(8,128)(2,1)}, u32[]{:S(2)}) copy-start(bf16[591,192]{0,1:T(8,128)(2,1)} %get-tuple-element.213) | copy-start | bytes 680836
  1953.3 1779.9 %all-to-all-start.10 = ((bf16[8,1,96]{2,1,0:T(2,128)(2,1)}), bf16[8,1,96]{2,1,0:T(2,128)(2,1)S(1)}, u32[]{:S(2)}, u32[]{:S(2)}) async-start(bf16[8,1,96]{2,1,0:T(2,128)(2,1)} %all_to_all.63), calls=%async_computation.10 | async-start | bytes 8192 | tf_op jit(solution)/shard_map/all_to_all | solution.py:22
  3733.2 9.6 all-to-all-start.11
  3742.8 9.6 all-to-all-start.7
  3752.5 9.6 all-to-all-start.9
  3762.1 9.6 all-to-all-start.8
  3771.8 9.6 all-to-all-start.6
  3775.1 9.8 copy-start.4
  3775.1 9.8 copy-start.41
  3775.1 9.8 copy-start.52
  3775.1 9.8 copy-start.54
  3781.4 12.6 all-to-all-start.1
  3794.0 13.1 copy-start.24
  3794.0 9.7 all-to-all-start.5
  3803.8 10.1 all-to-all-start.4
  3810.6 7.6 copy-start.2
  3810.6 7.6 copy-start.39
  3810.6 7.6 copy-start.44
  3810.6 7.6 copy-start.50
  3810.6 7.6 copy-start.66
  3813.9 31.5 all-to-all-start.3
  3821.8 28.5 copy-start.26
  3821.8 28.6 copy-start.37
  3821.8 28.6 copy-start.64
  3845.4 52.3 %all-to-all-start.2 = ((bf16[8,96,768]{2,1,0:T(8,128)(2,1)}), bf16[8,96,768]{2,1,0:T(8,128)(2,1)}, u32[]{:S(2)}, u32[]{:S(2)}) async-start(bf16[8,96,768]{2,1,0:T(8,128)(2,1)} %bitcast.239), calls=%async_computation.2 | async-start | bytes 2359296 | tf_op jit(solution)/shard_map/all_to_all | solution.py:22
  3856.0 48.2 %copy-start.8 = (f32[591,768]{1,0:T(8,128)S(1)}, f32[591,768]{1,0:T(8,128)}, u32[]{:S(2)}) copy-start(f32[591,768]{1,0:T(8,128)} %copy-done.7) | copy-start | bytes 5446660
  3897.7 22.1 all-to-all-start
  (23 other events, 40.8 us)
Sparse Core Ops, SparseCore 0:
  320.7 660.6 all-reduce.18
  1027.7 45.4 all-reduce.22
  1076.2 35.1 all-reduce.20
  1952.3 1815.3 all-reduce.24
Sparse Core Ops, SparseCore 1:
  323.2 654.9 all-gather.2
  980.3 40.0 all-gather.4
where the time goes:
time: 3960 us; the launch traced here: 3930 us
  starting transfers between devices  1830 us (46%)
  waiting for transfers between devices  827 us (21%)
  other arithmetic  664 us (17%)
  local copies, waits for them, and re-layouts  378 us (10%)
  blocking collectives  150 us (4%)
  matrix products  46.1 us (1%)
    all_to_all x12, starting transfers between devices, sent_and_summed(): lax.all_to_all(parts, axis, split_axis=0, concat_axis=0, tiled=True)  1810 us
    psum x1, waiting for transfers between devices, on_device(): branch = lax.psum(branch_part, 'shard') + vectors[2]  645 us
    scatter-add x1, other arithmetic, one_head(): return jax.ops.segment_sum(head_grads, flat_index, num_segments=table_size)  621 us
    gather x3, local copies, waits for them, and re-layouts, heads_forward(): pair_bias = jnp.take(table_rows, index_map, axis=1)  155 us
    gather x3, local copies, waits for them, and re-layouts, heads_backward(): pair_bias = jnp.take(table_rows, index_map, axis=1)  140 us
  transfers between devices with their start and end apart: 18, of which 15 were waited for; matrix products, arithmetic and copies ran while one was open for 1% of the time, Pallas kernels for 0%

commit v1 on v0

v1 whole, which is shorter than its diff:
```python
import functools

import jax
import jax.numpy as jnp
from jax import lax
from jax.experimental import pallas as pl
from jax.experimental.pallas import tpu as pltpu
from jax.sharding import PartitionSpec as P

HEAD_DIM = 64
SMALL_LEN = 197
LARGE_LEN = 577
EPS = 1e-06
NEG = -1e30
LANES = 128
SPLIT = 64
VMEM_LIMIT = 56 << 20

f32 = jnp.float32
bf16 = jnp.bfloat16


def up_to(value, unit):
    return -(-value // unit) * unit


def in_vmem(count):
    return [pl.BlockSpec(memory_space=pltpu.VMEM)] * count


def params(**more):
    return pltpu.CompilerParams(vmem_limit_bytes=VMEM_LIMIT, **more)


def dot(a, b, da, db):
    return lax.dot_general(a, b, (((da,), (db,)), ((), ())), preferred_element_type=f32)


def bias_body(heads, groups, index_ref, table_ref, out_ref):
    rows, columns = index_ref.shape

    def step(r, carry):
        here = pl.ds(pl.multiple_of(r * 16, 16), 16)
        for c in range(columns // LANES):
            there = pl.ds(c * LANES, LANES)
            index = index_ref[here, there]
            high = lax.shift_right_arithmetic(index, 7)
            low = lax.bitwise_and(index, LANES - 1)
            found = [jnp.full((16, LANES), NEG, f32) for _ in range(heads)]
            for k in range(groups):
                match = high == k
                for h in range(heads):
                    line = table_ref[h * groups + k : h * groups + k + 1, :]
                    values = jnp.take_along_axis(
                        jnp.broadcast_to(line, (16, LANES)), low, axis=1
                    )
                    found[h] = jnp.where(match, values, found[h])
            for h in range(heads):
                out_ref[h, here, there] = found[h].astype(bf16)
        return carry

    lax.fori_loop(0, rows // 16, step, 0)


def gather_bias(pair_index, table):
    heads, entries = table.shape
    groups = entries // LANES
    return pl.pallas_call(
        functools.partial(bias_body, heads, groups),
        out_shape=jax.ShapeDtypeStruct((heads,) + pair_index.shape, bf16),
        in_specs=in_vmem(2),
        out_specs=in_vmem(1)[0],
        compiler_params=params(),
        cost_estimate=pl.CostEstimate(flops=10**9, bytes_accessed=4 * 10**7, transcendentals=0),
        name="bias",
    )(pair_index, table.reshape(heads * groups, LANES))


def table_body(heads, groups, index_ref, grad_ref, out_ref):
    rows, columns = index_ref.shape
    shift = SPLIT.bit_length() - 1
    out_ref[...] = jnp.zeros_like(out_ref)

    def step(r, carry):
        here = pl.ds(pl.multiple_of(r * 16, 16), 16)
        index = index_ref[here, :]
        high = lax.shift_right_arithmetic(index, shift).astype(jnp.int16)
        low = lax.bitwise_and(index, SPLIT - 1).astype(jnp.int16)
        grads = [grad_ref[h, here, :] for h in range(heads)]
        places_low = lax.broadcasted_iota(jnp.int16, (SPLIT, columns), 0)
        places_high = lax.broadcasted_iota(jnp.int16, (groups, columns), 0)
        total = jnp.zeros(out_ref.shape, f32)
        for i in range(16):
            hot_low = jnp.where(
                places_low == jnp.broadcast_to(low[i : i + 1], (SPLIT, columns)),
                jnp.ones((), bf16),
                jnp.zeros((), bf16),
            )
            match = places_high == jnp.broadcast_to(high[i : i + 1], (groups, columns))
            spread = jnp.concatenate(
                [
                    jnp.where(
                        match,
                        jnp.broadcast_to(grads[h][i : i + 1], (groups, columns)),
                        jnp.zeros((), bf16),
                    )
                    for h in range(heads)
                ],
                0,
            )
            total = total + dot(spread, hot_low, 1, 1)
        out_ref[...] += total
        return carry

    lax.fori_loop(0, rows // 16, step, 0)


def table_sums(pair_index, grad_scores, entries):
    heads = grad_scores.shape[0]
    groups = up_to(-(-entries // SPLIT), 8)
    sums = pl.pallas_call(
        functools.partial(table_body, heads, groups),
        out_shape=jax.ShapeDtypeStruct((heads * groups, SPLIT), f32),
        in_specs=in_vmem(2),
        out_specs=in_vmem(1)[0],
        compiler_params=params(),
        cost_estimate=pl.CostEstimate(flops=2 * 10**9, bytes_accessed=6 * 10**7, transcendentals=0),
        name="table_sums",
    )(pair_index, grad_scores)
    return sums.reshape(heads, groups * SPLIT)


def forward_body(heads, q_ref, k_ref, v_ref, bias_ref, out_ref):
    rows = q_ref.shape[0]
    for h in range(heads):
        part = slice(h * HEAD_DIM, (h + 1) * HEAD_DIM)
        scores = dot(q_ref[:, part], k_ref[:, part], 1, 1) * HEAD_DIM ** (-0.5)
        scores = scores + bias_ref[h, :, :rows].astype(f32)
        weights = jnp.exp(scores - jnp.max(scores, -1, keepdims=True))
        weights = weights / jnp.sum(weights, -1, keepdims=True)
        out_ref[:, part] = dot(weights.astype(bf16), v_ref[:, part], 1, 0).astype(bf16)


def backward_body(
    heads, q_ref, k_ref, v_ref, bias_ref, grad_ref, dq_ref, dk_ref, dv_ref, ds_ref
):
    rows = q_ref.shape[0]
    factor = HEAD_DIM ** (-0.5)
    for h in range(heads):
        part = slice(h * HEAD_DIM, (h + 1) * HEAD_DIM)
        scores = dot(q_ref[:, part], k_ref[:, part], 1, 1) * factor
        scores = scores + bias_ref[h, :, :rows].astype(f32)
        weights = jnp.exp(scores - jnp.max(scores, -1, keepdims=True))
        weights = weights / jnp.sum(weights, -1, keepdims=True)
        dv_ref[:, part] = dot(weights.astype(bf16), grad_ref[:, part], 0, 0).astype(bf16)
        grad = dot(grad_ref[:, part], v_ref[:, part], 1, 1)
        mean = jnp.sum(weights * grad, -1, keepdims=True)
        grad = (weights * (grad - mean)).astype(bf16)
        ds_ref[h, :, :rows] = grad
        dq_ref[:, part] = (dot(grad, k_ref[:, part], 1, 0) * factor).astype(bf16)
        dk_ref[:, part] = (dot(grad, q_ref[:, part], 0, 0) * factor).astype(bf16)


def attend_forward(queries, keys, values, bias):
    heads = bias.shape[0]
    return pl.pallas_call(
        functools.partial(forward_body, heads),
        out_shape=jax.ShapeDtypeStruct(queries.shape, bf16),
        in_specs=in_vmem(4),
        out_specs=in_vmem(1)[0],
        compiler_params=params(),
        cost_estimate=pl.CostEstimate(flops=10**9, bytes_accessed=10**7, transcendentals=10**6),
        name="attend_forward",
    )(queries, keys, values, bias)


def attend_backward(queries, keys, values, bias, grad):
    heads = bias.shape[0]
    rows = jax.ShapeDtypeStruct(queries.shape, bf16)
    return pl.pallas_call(
        functools.partial(backward_body, heads),
        out_shape=(rows, rows, rows, jax.ShapeDtypeStruct(bias.shape, bf16)),
        in_specs=in_vmem(5),
        out_specs=tuple(in_vmem(4)),
        compiler_params=params(),
        cost_estimate=pl.CostEstimate(flops=2 * 10**9, bytes_accessed=2 * 10**7, transcendentals=10**6),
        name="attend_backward",
    )(queries, keys, values, bias, grad)


def layer_norm(activations, norm_gain, norm_shift):
    center = activations - jnp.mean(activations, -1, keepdims=True)
    inverse = lax.rsqrt(jnp.mean(center * center, -1, keepdims=True) + EPS)
    normal = center * inverse
    return (normal * norm_gain + norm_shift, normal, inverse)


def norm_back(grad_normed, normal, inverse, norm_gain):
    scaled = grad_normed * norm_gain
    return inverse * (
        scaled
        - jnp.mean(scaled, -1, keepdims=True)
        - normal * jnp.mean(scaled * normal, -1, keepdims=True)
    )


def gelu_slope(hidden):
    cumulative = 0.5 * (1.0 + jax.scipy.special.erf(hidden * 0.7071067811865476))
    return cumulative + hidden * jnp.exp(-0.5 * hidden * hidden) * 0.3989422804014327


def pair_map(kind, small_index, large_index, rows, columns):
    length = small_index.shape[0]
    images = rows // length
    tiled = jnp.tile(small_index, (images, images))
    tiled = jnp.pad(
        tiled,
        ((0, rows - images * length), (0, columns - images * length)),
        constant_values=-1,
    )
    image_row = jnp.arange(rows) // length
    image_column = jnp.arange(columns) // length
    tiled = jnp.where(image_row[:, None] == image_column[None, :], tiled, -1)
    side = large_index.shape[0]
    large = jnp.pad(
        large_index, ((0, rows - side), (0, columns - side)), constant_values=-1
    )
    return jnp.where(kind == 1, large, tiled)


def on_device(
    images,
    out_grad,
    slot_kind,
    small_index,
    large_index,
    qkv_weight,
    out_weight,
    fc1_weight,
    fc2_weight,
    norm1_gain,
    norm1_shift,
    query_bias,
    value_bias,
    out_bias,
    gamma_attn,
    norm2_gain,
    norm2_shift,
    fc1_bias,
    fc2_bias,
    gamma_mlp,
    small_table,
    large_table,
):
    depth = qkv_weight.shape[0]
    width = query_bias.shape[0]
    hidden_width = fc1_bias.shape[0]
    heads = width // HEAD_DIM
    _, slot_rows, model_width = images.shape
    rows = up_to(slot_rows, 16)
    columns = up_to(rows, LANES)
    kind = slot_kind[0]

    block = jnp.concatenate(
        (
            qkv_weight.reshape(depth, 3 * width),
            fc1_weight,
            out_weight.T,
            fc2_weight.T,
        ),
        1,
    )
    whole = lax.all_gather(block, "dp", axis=0, tiled=True)
    cuts = (3 * width, 3 * width + hidden_width, 4 * width + hidden_width)
    qkv_matrix = whole[:, : cuts[0]]
    fc1_matrix = whole[:, cuts[0] : cuts[1]]
    out_turned = whole[:, cuts[1] : cuts[2]]
    fc2_turned = whole[:, cuts[2] :]
    small_vectors = jnp.stack(
        (norm1_gain, norm1_shift, out_bias, gamma_attn, norm2_gain, norm2_shift, fc2_bias, gamma_mlp)
    )
    vectors = lax.all_gather(small_vectors, "dp", axis=0)
    vectors = jnp.moveaxis(vectors, 0, 1).reshape(8, model_width).astype(f32)

    query_shift = query_bias.astype(f32)
    value_shift = value_bias.astype(f32)
    hidden_shift = fc1_bias.astype(f32)
    small_entries, large_entries = small_table.shape[0], large_table.shape[0]
    entries = up_to(max(small_entries, large_entries), LANES)
    table = jnp.where(
        kind == 1,
        jnp.pad(large_table, ((0, entries - large_entries), (0, 0))),
        jnp.pad(small_table, ((0, entries - small_entries), (0, 0))),
    )
    table = table.T.astype(f32)
    pair_index = pair_map(kind, small_index, large_index, rows, columns)
    bias = gather_bias(pair_index, table)

    positions = jnp.arange(rows)
    live_count = jnp.where(kind == 1, LARGE_LEN, slot_rows)
    live_rows = (positions < live_count).astype(f32).reshape(-1, 1)
    inputs = jnp.pad(images[0], ((0, rows - slot_rows), (0, 0))).astype(f32)
    normed_one, normal_one, inverse_one = layer_norm(inputs, vectors[0], vectors[1])
    normed_one = normed_one.astype(bf16)
    projected = dot(normed_one, qkv_matrix, 1, 0)
    queries = (projected[:, :width] + query_shift).astype(bf16)
    keys = projected[:, width : 2 * width].astype(bf16)
    values = (projected[:, 2 * width :] + value_shift).astype(bf16)
    pieces = attend_forward(queries, keys, values, bias)
    branch_part = dot(pieces, out_turned, 1, 1)
    branch = lax.psum(branch_part, "shard") + vectors[2]
    middle = inputs + vectors[3] * branch
    normed_two, normal_two, inverse_two = layer_norm(middle, vectors[4], vectors[5])
    normed_two = normed_two.astype(bf16)
    hidden = dot(normed_two, fc1_matrix, 1, 0) + hidden_shift
    active = jax.nn.gelu(hidden, approximate=False).astype(bf16)
    result_part = dot(active, fc2_turned, 1, 1)
    result = lax.psum(result_part.astype(bf16), "shard").astype(f32) + vectors[6]
    layer_out = ((middle + vectors[7] * result) * live_rows).astype(bf16)[:slot_rows][None]

    grad_out = jnp.pad(out_grad[0], ((0, rows - slot_rows), (0, 0))).astype(f32) * live_rows
    grad_gamma_mlp = jnp.sum(grad_out * result, 0)
    grad_result = (grad_out * vectors[7]).astype(bf16)
    grad_fc2_bias = jnp.sum(grad_result.astype(f32), 0)
    grad_fc2_turned = dot(grad_result, active, 0, 0)
    grad_active = dot(grad_result, fc2_turned, 1, 0)
    grad_hidden = (grad_active * gelu_slope(hidden)).astype(bf16)
    grad_fc1_bias = jnp.sum(grad_hidden.astype(f32), 0)
    grad_fc1 = dot(normed_two, grad_hidden, 0, 0)
    grad_normed_two = lax.psum(dot(grad_hidden, fc1_matrix, 1, 1), "shard")
    grad_norm2_gain = jnp.sum(grad_normed_two * normal_two, 0)
    grad_norm2_shift = jnp.sum(grad_normed_two, 0)
    grad_middle = grad_out + norm_back(grad_normed_two, normal_two, inverse_two, vectors[4])
    grad_gamma_attn = jnp.sum(grad_middle * branch, 0)
    grad_branch = (grad_middle * vectors[3]).astype(bf16)
    grad_out_bias = jnp.sum(grad_branch.astype(f32), 0)
    grad_out_turned = dot(grad_branch, pieces, 0, 0)
    grad_attended = dot(grad_branch, out_turned, 1, 0).astype(bf16)
    grad_queries, grad_keys, grad_values, grad_scores = attend_backward(
        queries, keys, values, bias, grad_attended
    )
    sums = table_sums(pair_index, grad_scores, entries)
    grad_projected = jnp.concatenate((grad_queries, grad_keys, grad_values), 1)
    grad_qkv = dot(normed_one, grad_projected, 0, 0)
    grad_query_bias = jnp.sum(grad_queries.astype(f32), 0)
    grad_value_bias = jnp.sum(grad_values.astype(f32), 0)
    grad_normed_one = lax.psum(dot(grad_projected, qkv_matrix, 1, 1), "shard")
    grad_norm1_gain = jnp.sum(grad_normed_one * normal_one, 0)
    grad_norm1_shift = jnp.sum(grad_normed_one, 0)
    input_grad = grad_middle + norm_back(grad_normed_one, normal_one, inverse_one, vectors[0])
    input_grad = input_grad.astype(bf16)[:slot_rows][None]

    small_sums = jnp.where(kind == 1, 0.0, sums[:, :small_entries])
    large_sums = jnp.where(kind == 1, sums[:, :large_entries], 0.0)
    local_sums = lax.psum(
        (small_sums, large_sums, grad_query_bias, grad_value_bias, grad_fc1_bias), "dp"
    )
    peers = lax.axis_size("dp")

    def sent_and_summed(value):
        parts = value.astype(bf16).reshape(peers, value.shape[0] // peers, -1)
        arrived = lax.all_to_all(parts, "dp", split_axis=0, concat_axis=0, tiled=True)
        return arrived.astype(f32).sum(axis=0)

    grad_block = sent_and_summed(
        jnp.concatenate((grad_qkv, grad_fc1, grad_out_turned, grad_fc2_turned), 1)
    )
    vector_grads = sent_and_summed(
        jnp.stack(
            (
                grad_norm1_gain,
                grad_norm1_shift,
                grad_out_bias,
                grad_gamma_attn,
                grad_norm2_gain,
                grad_norm2_shift,
                grad_fc2_bias,
                grad_gamma_mlp,
            ),
            1,
        )
    )
    return (
        layer_out,
        input_grad,
        grad_block[:, : cuts[0]].reshape(depth, 3, width),
        grad_block[:, cuts[1] : cuts[2]].T,
        grad_block[:, cuts[0] : cuts[1]],
        grad_block[:, cuts[2] :].T,
        vector_grads[:, 0],
        vector_grads[:, 1],
        local_sums[2],
        local_sums[3],
        vector_grads[:, 2],
        vector_grads[:, 3],
        vector_grads[:, 4],
        vector_grads[:, 5],
        local_sums[4],
        vector_grads[:, 6],
        vector_grads[:, 7],
        local_sums[0].T,
        local_sums[1].T,
    )


def solution(mesh):
    return jax.shard_map(
        on_device,
        mesh=mesh,
        in_specs=(
            P("dp", None, None),
            P("dp", None, None),
            P("dp"),
            P(),
            P(),
            P("dp", None, "shard"),
            P("shard", "dp"),
            P("dp", "shard"),
            P("shard", "dp"),
            P("dp"),
            P("dp"),
            P("shard"),
            P("shard"),
            P("dp"),
            P("dp"),
            P("dp"),
            P("dp"),
            P("shard"),
            P("dp"),
            P("dp"),
            P(None, "shard"),
            P(None, "shard"),
        ),
        out_specs=(
            P("dp", None, None),
            P("dp", None, None),
            P("dp", None, "shard"),
            P("shard", "dp"),
            P("dp", "shard"),
            P("shard", "dp"),
            P("dp"),
            P("dp"),
            P("shard"),
            P("shard"),
            P("dp"),
            P("dp"),
            P("dp"),
            P("dp"),
            P("shard"),
            P("dp"),
            P("dp"),
            P(None, "shard"),
            P(None, "shard"),
        ),
        check_vma=False,
    )
```

time: 3960 us -> 456 us (0.12)
  starting transfers between devices: 1830 us -> 11.9 us
  waiting for transfers between devices: 827 us -> 167 us
  other arithmetic: 664 us -> 28.2 us
  local copies, waits for them, and re-layouts: 378 us -> 29 us
  Pallas kernels: 0 us -> 73.2 us
  blocking collectives: 150 us -> 95.5 us
    all_to_all x12 -> x2, starting transfers between devices: 1810 us -> 11.5 us  [sent_and_summed(): lax.all_to_all(parts, 'dp', split_axis=0, concat_axis=0, tiled=True)]
    scatter-add x1 -> x0, other arithmetic: 621 us -> none  [one_head(): return jax.ops.segment_sum(head_grads, flat_index, num_segments=table_size)]
    psum x1, waiting for transfers between devices: 645 us -> 45.1 us  [on_device(): branch = lax.psum(branch_part, 'shard') + vectors[2]]
    gather x6 -> x0, local copies, waits for them, and re-layouts: 295 us -> none  [the longest x3 155 us: heads_forward(): pair_bias = jnp.take(table_rows, index_map, axis=1)]
    all_to_all x12 -> x2, waiting for transfers between devices: 76.9 us -> 0.01 us  [sent_and_summed(): lax.all_to_all(parts, 'dp', split_axis=0, concat_axis=0, tiled=True)]
    pallas_call x0 -> x4, Pallas kernels: none -> 73.2 us  [the longest x1 34.1 us: table_sums(): pl.pallas_call(functools.partial(table_body, heads, groups), out_shape=ja...]
    all_gather x2 -> x1, blocking collectives: 71.3 us -> 27.9 us  [on_device(): vectors = lax.all_gather(small_vectors, 'dp', axis=0)]
    convert_element_type x17 -> x1, local copies, waits for them, and re-layouts: 41.5 us -> 0.88 us  [on_device(): grad_attended = dot(grad_branch, out_turned, 1, 0).astype(bf16)]
  transfers between devices with their start and end apart: 18 -> 7, of which waited for: 15 -> 5; matrix products, arithmetic and copies ran while one was open for 1% -> 10% of each run, Pallas kernels for 0% -> 13%
where the time goes in v1:
time: 456 us; the launch traced here: 454 us
  waiting for transfers between devices  167 us (37%)
  blocking collectives  95.5 us (21%)
  Pallas kernels  73.2 us (16%)
  matrix products  34.7 us (8%)
  local copies, waits for them, and re-layouts  29 us (6%)
  other arithmetic  28.2 us (6%)
  between operations  14.9 us (3%)
  starting transfers between devices  11.9 us (3%)
    psum x1, blocking collectives, on_device(): lax.psum((small_sums, large_sums, grad_query_bias, grad_value_bias, grad_...  67.6 us
    psum x1, waiting for transfers between devices, on_device(): branch = lax.psum(branch_part, 'shard') + vectors[2]  45.1 us
    psum x1, waiting for transfers between devices, on_device(): grad_normed_two = lax.psum(dot(grad_hidden, fc1_matrix, 1, 1), 'shard')  43.6 us
    psum x1, waiting for transfers between devices, on_device(): grad_normed_one = lax.psum(dot(grad_projected, qkv_matrix, 1, 1), 'shard')  36 us
    psum x1, waiting for transfers between devices, on_device(): lax.psum(result_part.astype(bf16), 'shard').astype(f32) + vectors[6]  35.6 us
    dot_general x12, matrix products, dot(): lax.dot_general(a, b, (((da,), (db,)), ((), ())), preferred_element_type=...  34.7 us
    pallas_call x1, Pallas kernels, table_sums(): pl.pallas_call(functools.partial(table_body, heads, groups), out_shape=ja...  34.1 us
    all_gather x1, blocking collectives, on_device(): vectors = lax.all_gather(small_vectors, 'dp', axis=0)  27.9 us
  transfers between devices with their start and end apart: 7, of which 5 were waited for; matrix products, arithmetic and copies ran while one was open for 10% of the time, Pallas kernels for 13%

profile of v1, /device:TPU:0, one launch (start us, length us, event | category | flops | bytes accessed | tf_op | source)
XLA Modules:
  0.0 454.5 jit_solution(10214068676710384523)
XLA Ops:
  7.4 1.2 copy.75
  8.5 0.2 copy.77
  8.7 0.9 copy.76
  9.6 1.9 concatenate.21
  11.7 27.9 %all-gather = bf16[64,96]{1,0:T(8,128)(2,1)S(1)} all-gather(bf16[8,96]{1,0:T(8,128)(2,1)S(1)} %stack.62), channel_id=2, replica_groups=mesh['dp'=8,'shard'=4] {'dp'}, dimensions={0}, use_global_device_ids=true | all-gather | bytes 13824 | tf_op jit(solution)/shard_map/all_gather | solution.py:282
  40.6 0.3 tile.4
  40.9 2.5 tile.10
  43.4 0.6 reshape.188.table_ref
  44.1 0.2 convert_reduce_fusion.1
  44.3 3.6 select_select_fusion.index_ref
  47.9 24.8 %bias.1.bias_ref = bf16[3,592,640]{2,1,0:T(8,128)(2,1)} custom-call(s32[592,640]{1,0:T(8,128)} %select_select_fusion.index_ref, f32[54,128]{1,0:T(8,128)} %reshape.188.table_ref), custom_call_target="tpu_custom_call" | custom-call | flops 1000000000 | bytes 40000000 | tf_op jit(solution)/shard_map/bias/pallas_call | solution.py:68
  72.6 0.4 fusion.2
  73.0 6.7 %all-gather.3.cloned.1.call-done = bf16[768,2304]{1,0:T(8,128)(2,1)} async-done(((bf16[96,2304]{1,0:T(8,128)(2,1)}), bf16[768,2304]{1,0:T(8,128)(2,1)}) %all-gather.3.cloned.1.call-update) | async-done | bytes 3538960 | tf_op jit(solution)/shard_map/all_gather | solution.py:273
  79.7 2.3 fusion.34
  82.1 0.2 copy.89
  82.4 0.2 copy.91
  82.6 0.9 copy.90.k_ref
  83.5 1.0 add_convert_fusion.2
  84.5 5.4 %attend_forward.1 = bf16[592,192]{1,0:T(8,128)(2,1)} custom-call(bf16[592,192]{1,0:T(8,128)(2,1)} %get-tuple-element.156.q_ref, bf16[592,192]{1,0:T(8,128)(2,1)} %copy.90.k_ref, bf16[592,192]{1,0:T(8,128)(2,1)} %get-tuple-element.155.v_ref, bf16[3,592,640]{2,1,0:T(8,128)(2,1)} %bias.1.bias_ref), custom_call_target="tpu_custom_call" | custom-call | flops 1000000000 | bytes 10000000 | tf_op jit(solution)/shard_map/attend_forward/pallas_call | solution.py:166
  89.9 3.0 fusion.37
  92.9 0.2 all-reduce.16.cloned.1.call-start
  93.5 45.1 %all-reduce.12.cloned.1.call-done = f32[592,768]{1,0:T(8,128)} async-done(((f32[592,768]{1,0:T(8,128)}), f32[592,768]{1,0:T(8,128)}) %all-reduce.12.cloned.1.call-update) | async-done | bytes 1818640 | tf_op jit(solution)/shard_map/psum | solution.py:311
  138.6 2.0 fusion.56
  140.6 0.3 multiply_reduce_fusion.6
  141.1 5.8 %fusion.5 = (bf16[592,768]{1,0:T(8,128)(2,1)}, f32[592,768]{1,0:T(8,128)S(1)}) fusion(f32[768]{0:T(1024)S(1)} %convert_element_type.115, bf16[768,2304]{1,0:T(8,128)(2,1)S(1)} %copy-done.11, f32[592,768]{1,0:T(8,128)S(1)} %get-tuple-element.130, f32[768]{0:T(1024)S(1)} %add.151, f32[768]{0:T(1024)S(1)} %mul.196, f32[592]{0:T(1024)S(1)} %add_rsqrt_fusion, ...), kind=kOutput, calls=%fused_computation.11 | convolution fusion | flops 730632192 | bytes 5746688 | tf_op jit(solution)/shard_map/dot_general | solution.py:36
  147.0 1.4 convert_reduce_fusion.2
  148.4 1.0 copy-done.25
  149.4 2.3 fusion.26
  151.9 3.4 convolution_convert_fusion.2
  155.3 43.6 %all-reduce.16.cloned.1.call-done = f32[592,768]{1,0:T(8,128)} async-done(((f32[592,768]{1,0:T(8,128)}), f32[592,768]{1,0:T(8,128)}) %all-reduce.16.cloned.1.call-update) | async-done | bytes 1818640 | tf_op jit(solution)/shard_map/psum | solution.py:330
  198.9 2.3 multiply_reduce_fusion.1
  201.3 35.6 %all-reduce.14.cloned.1.call-done = bf16[592,768]{1,0:T(8,128)(2,1)} async-done(((bf16[592,768]{1,0:T(8,128)(2,1)}), bf16[592,768]{1,0:T(8,128)(2,1)}) %all-reduce.14.cloned.1.call-update) | async-done | bytes 909328 | tf_op jit(solution)/shard_map/psum | solution.py:318
  236.9 4.1 multiply_reduce_fusion
  241.1 1.3 copy-done
  242.3 0.2 fusion.55
  242.6 0.9 copy-done.3
  243.5 1.8 convolution_convert_fusion.5
  245.3 0.9 copy.81.grad_ref
  246.2 8.9 %attend_backward.1 = (bf16[592,192]{1,0:T(8,128)(2,1)}, bf16[592,192]{1,0:T(8,128)(2,1)}, bf16[592,192]{1,0:T(8,128)(2,1)}, bf16[3,592,640]{2,1,0:T(8,128)(2,1)}) custom-call(bf16[592,192]{1,0:T(8,128)(2,1)} %get-tuple-element.156.q_ref, bf16[592,192]{1,0:T(8,128)(2,1)} %copy.90.k_ref, bf16[592,192]{1,0:T(8,128)(2,1)} %get-tuple-element.155.v_ref, ...), custom_call_target="tpu_custom_call" | custom-call | flops 2000000000 | bytes 20000000 | tf_op jit(solution)/shard_map/attend_backward/pallas_call | solution.py:180
  255.1 3.6 fusion.32
  258.7 1.5 fusion.50
  260.3 3.9 convolution_convert_fusion
  264.2 2.4 convolution_convert_fusion.1
  267.0 3.2 convolution_convert_fusion.3
  270.3 36.0 %all-reduce.18.cloned.1.call-done = f32[592,768]{1,0:T(8,128)} async-done(((f32[592,768]{1,0:T(8,128)}), f32[592,768]{1,0:T(8,128)}) %all-reduce.18.cloned.1.call-update) | async-done | bytes 1818640 | tf_op jit(solution)/shard_map/psum | solution.py:347
  306.2 3.8 fusion.53
  310.3 0.6 copy.85
  310.9 5.5 %all-to-all-start.1 = ((bf16[8,96,8]{1,2,0:T(8,128)(2,1)}), bf16[8,96,8]{1,2,0:T(8,128)(2,1)S(1)}, u32[]{:S(2)}, u32[]{:S(2)}) async-start(bf16[8,96,8]{1,2,0:T(8,128)(2,1)} %copy.85), calls=%async_computation.1 | async-start | bytes 32768 | tf_op jit(solution)/shard_map/all_to_all | solution.py:362
  316.4 1.6 convolution_convert_fusion.4
  318.1 0.2 copy.88
  318.2 2.2 copy.82
  320.5 7.0 %concatenate.27 = bf16[8,96,2304]{2,1,0:T(8,128)(2,1)} concatenate(bf16[8,96,576]{2,1,0:T(8,128)(2,1)} %bitcast.72, bf16[8,96,768]{2,1,0:T(8,128)(2,1)} %bitcast.79, bf16[8,96,192]{2,1,0:T(8,128)(2,1)S(1)} %bitcast.77, bf16[8,96,768]{2,1,0:T(8,128)(2,1)} %bitcast.78), dimensions={2} | concatenate | bytes 7077888 | tf_op jit(solution)/shard_map/concatenate | solution.py:366
  327.4 6.0 %all-to-all-start = ((bf16[8,96,2304]{2,1,0:T(8,128)(2,1)}), bf16[8,96,2304]{2,1,0:T(8,128)(2,1)}, u32[]{:S(2)}, u32[]{:S(2)}) async-start(bf16[8,96,2304]{2,1,0:T(8,128)(2,1)} %concatenate.27), calls=%async_computation | async-start | bytes 7077888 | tf_op jit(solution)/shard_map/all_to_all | solution.py:362
  333.4 34.1 %table_sums.1 = f32[120,64]{1,0:T(8,128)} custom-call(s32[592,640]{1,0:T(8,128)} %select_select_fusion.index_ref, bf16[3,592,640]{2,1,0:T(8,128)(2,1)} %get-tuple-element.26.grad_ref), custom_call_target="tpu_custom_call" | custom-call | flops 2000000000 | bytes 60000000 | tf_op jit(solution)/shard_map/table_sums/pallas_call | solution.py:121
  367.5 0.9 reshape.186
  368.7 67.6 %all-reduce.6 = (f32[192]{0:T(256)}, f32[192]{0:T(256)}, f32[768]{0:T(1024)}, f32[732,3]{0,1:T(4,128)}, f32[2212,3]{0,1:T(4,128)}) all-reduce(f32[192]{0:T(256)S(1)} %convert_reduce_fusion.4, f32[192]{0:T(256)S(1)} %convert_reduce_fusion.3, f32[768]{0:T(1024)S(1)} %get-tuple-element.153, ...), channel_id=1, replica_groups=mesh['dp'=8,'shard'=4] {'dp'}, use_global_device_ids=true, to_apply=%region_23.24 | all-reduce | flops 9984 | bytes 79872 | tf_op jit(solution)/shard_map/psum | solution.py:355
  436.3 2.9 fusion.30
  439.2 2.9 fusion.31
  442.1 0.5 slice_bitcast_fusion.2
  442.6 2.6 convert_reduce_fusion
  445.2 0.9 slice_bitcast_fusion
  446.2 0.2 copy.84
  446.3 0.9 copy.86
  447.2 0.7 copy.87
  (113 shorter events, 2.5 us)
Async XLA Ops:
  7.2 4.4 copy-start.15
  7.2 4.4 copy-start.16
  7.2 4.4 copy-start.17
  7.2 4.4 copy-start.18
  7.2 4.4 copy-start.19
  7.2 4.4 copy-start.20
  7.3 4.4 copy-start.21
  7.3 4.4 copy-start.22
  7.3 32.6 %copy-start.23 = (bf16[192]{0:T(256)(128)(2,1)S(1)}, bf16[192]{0:T(256)(128)(2,1)}, u32[]{:S(2)}) copy-start(bf16[192]{0:T(256)(128)(2,1)} %param.33) | copy-start | bytes 1156
  7.3 32.6 %copy-start.24 = (bf16[192]{0:T(256)(128)(2,1)S(1)}, bf16[192]{0:T(256)(128)(2,1)}, u32[]{:S(2)}) copy-start(bf16[192]{0:T(256)(128)(2,1)} %param.34) | copy-start | bytes 1156
  7.3 33.2 %copy-start.10 = (s32[197,197]{1,0:T(8,128)S(1)}, s32[197,197]{1,0:T(8,128)}, u32[]{:S(2)}) copy-start(s32[197,197]{1,0:T(8,128)} %param.25) | copy-start | bytes 465712
  7.3 72.4 %all-gather.3.cloned.1.call-start = ((), (), s32[]{:S(2)}) async-start(), calls=%async_computation.2 | async-start | bytes 3981312 | tf_op jit(solution)/shard_map/all_gather | solution.py:273
  11.5 127.0 %all-reduce.12.cloned.1.call-start = ((), (), s32[]{:S(2)}) async-start(), calls=%async_computation.3 | async-start | bytes 3637248 | tf_op jit(solution)/shard_map/psum | solution.py:311
  40.9 2.5 copy-start.12
  40.9 2.5 copy-start.13
  40.9 3.2 copy-start.2
  89.9 3.5 copy-start.14
  92.9 106.1 %all-reduce.16.cloned.1.call-start = ((), (), s32[]{:S(2)}) async-start(), calls=%async_computation.5 | async-start | bytes 3637248 | tf_op jit(solution)/shard_map/psum | solution.py:330
  138.6 2.5 copy-start.11
  141.1 5.9 %copy-start.5 = (bf16[1,591,768]{2,1,0:T(8,128)(2,1)S(1)}, bf16[1,591,768]{2,1,0:T(8,128)(2,1)}, u32[]{:S(2)}) copy-start(bf16[1,591,768]{2,1,0:T(8,128)(2,1)} %param.23) | copy-start | bytes 2723332
  148.4 1.0 copy-start.25
  151.7 85.2 %all-reduce.14.cloned.1.call-start = ((), (), s32[]{:S(2)}) async-start(), calls=%async_computation.4 | async-start | bytes 1818624 | tf_op jit(solution)/shard_map/psum | solution.py:318
  155.3 151.0 %all-reduce.18.cloned.1.call-start = ((), (), s32[]{:S(2)}) async-start(), calls=%async_computation.6 | async-start | bytes 3637248 | tf_op jit(solution)/shard_map/psum | solution.py:347
  241.1 1.3 copy-start
  242.6 0.9 copy-start.3
  260.3 3.9 copy-start.26
  264.2 2.9 copy-start.7
  264.2 2.9 copy-start.8
  270.3 46.2 %copy-start.6 = (bf16[592,192]{1,0:T(8,128)(2,1)S(1)}, bf16[592,192]{1,0:T(8,128)(2,1)}, u32[]{:S(2)}) copy-start(bf16[592,192]{1,0:T(8,128)(2,1)} %attend_forward.1) | copy-start | bytes 681988
  310.9 16.5 %all-to-all-start.1 = ((bf16[8,96,8]{1,2,0:T(8,128)(2,1)}), bf16[8,96,8]{1,2,0:T(8,128)(2,1)S(1)}, u32[]{:S(2)}, u32[]{:S(2)}) async-start(bf16[8,96,8]{1,2,0:T(8,128)(2,1)} %copy.85), calls=%async_computation.1 | async-start | bytes 32768 | tf_op jit(solution)/shard_map/all_to_all | solution.py:362
  327.4 115.2 %all-to-all-start = ((bf16[8,96,2304]{2,1,0:T(8,128)(2,1)}), bf16[8,96,2304]{2,1,0:T(8,128)(2,1)}, u32[]{:S(2)}, u32[]{:S(2)}) async-start(bf16[8,96,2304]{2,1,0:T(8,128)(2,1)} %concatenate.27), calls=%async_computation | async-start | bytes 7077888 | tf_op jit(solution)/shard_map/all_to_all | solution.py:362
  333.4 35.0 %copy-start.9 = (bf16[592,192]{1,0:T(8,128)(2,1)S(1)}, bf16[592,192]{1,0:T(8,128)(2,1)}, u32[]{:S(2)}) copy-start(bf16[592,192]{1,0:T(8,128)(2,1)} %get-tuple-element.25) | copy-start | bytes 681988
  436.3 2.9 copy-start.1
  436.3 2.9 copy-start.4
Sparse Core Ops, SparseCore 0:
  11.7 68.0 all-gather.2
  93.0 45.5 all-reduce.11
  151.9 47.0 all-reduce.15
  201.8 35.1 all-reduce.13
  258.8 47.3 all-reduce.17

commit v2 on v1

--- a/solution.py
+++ b/solution.py
@@ -15,6 +15,8 @@
 LANES = 128
 SPLIT = 64
 VMEM_LIMIT = 56 << 20
+
+MESH = pl.DeviceIdType.MESH
 
 f32 = jnp.float32
 bf16 = jnp.bfloat16
@@ -188,6 +190,135 @@
     )(queries, keys, values, bias, grad)
 
 
+def cuts_of(total, pieces, unit=16):
+    n=total//unit; base,extra=divmod(n,pieces)
+    out=[];at=0
+    for i in range(pieces):
+        size=(base+(i<extra))*unit
+        if size: out.append((at,size))
+        at+=size
+    return out
+
+def shard_sum_body(chunks, part_ref, out_ref, near, sent, far, send_sem, recv_sem):
+    me=lax.axis_index("shard")
+    outer=me//2; inner=lax.rem(me,2)
+    near_peer=outer*2+(1-inner); far_peer=(1-outer)*2+inner
+    barrier=pltpu.get_barrier_semaphore()
+    for peer in (near_peer,far_peer):
+        pl.semaphore_signal(barrier,inc=1,device_id={"shard":peer},device_id_type=MESH)
+    pl.semaphore_wait(barrier,2)
+    half=near.shape[0]
+    def rows(which,at,size):
+        return pl.ds(pl.multiple_of(which*half+at,16),size)
+    def copy(stage,j,src,dst,peer):
+        return pltpu.make_async_remote_copy(src_ref=src,dst_ref=dst,send_sem=send_sem.at[stage,j],recv_sem=recv_sem.at[stage,j],device_id={"shard":peer},device_id_type=MESH)
+    first=[];second=[];third=[]
+    for j,(at,size) in enumerate(chunks):
+        c=copy(0,j,part_ref.at[rows(1-inner,at,size)],near.at[pl.ds(at,size)],near_peer); c.start(); first.append(c)
+    for j,(at,size) in enumerate(chunks):
+        first[j].wait_recv()
+        here=pl.ds(at,size)
+        sent[here]=(part_ref[rows(inner,at,size)]+near[here]).astype(bf16)
+        c=copy(1,j,sent.at[here],far.at[here],far_peer); c.start(); second.append(c)
+    for j,(at,size) in enumerate(chunks):
+        second[j].wait_recv()
+        here=pl.ds(at,size)
+        mine=rows(inner,at,size)
+        out_ref[mine]=sent[here].astype(f32)+far[here].astype(f32)
+        c=copy(2,j,out_ref.at[mine],out_ref.at[mine],near_peer); c.start(); third.append(c)
+    for j in range(len(chunks)):
+        first[j].wait_send(); second[j].wait_send(); third[j].wait()
+
+def shard_sum(part, pieces=4, cid=0):
+    rows,width=part.shape
+    half=rows//2
+    chunks=cuts_of(half,pieces)
+    return pl.pallas_call(functools.partial(shard_sum_body,chunks),
+        out_shape=jax.ShapeDtypeStruct(part.shape,f32),
+        in_specs=[pl.BlockSpec(memory_space=pltpu.VMEM)],out_specs=pl.BlockSpec(memory_space=pltpu.VMEM),
+        scratch_shapes=[pltpu.VMEM((half,width),f32),pltpu.VMEM((half,width),bf16),pltpu.VMEM((half,width),bf16),
+            pltpu.SemaphoreType.DMA((3,len(chunks))),pltpu.SemaphoreType.DMA((3,len(chunks)))],
+        compiler_params=pltpu.CompilerParams(collective_id=cid,has_side_effects=True,vmem_limit_bytes=VMEM_LIMIT),name="shard_sum%d"%pieces)(part)
+
+def gather_body(blocks, *refs):
+    n=blocks
+    ins=refs[:n]; outs=refs[n:2*n]; loc,up_s,up_r,dn_s,dn_r,x_s,x_r=refs[2*n:]
+    X=2
+    dp=outs[0].shape[0]; Z=dp//X
+    me=lax.axis_index("dp"); z=me//X; x=lax.rem(me,X)
+    barrier=pltpu.get_barrier_semaphore()
+    up=me+X; dn=me-X; xp=z*X+(1-x)
+    has_up=z<Z-1; has_dn=z>0
+    def sig(p): pl.semaphore_signal(barrier,inc=1,device_id={"dp":p},device_id_type=MESH)
+    sig(xp)
+    @pl.when(has_up)
+    def _(): sig(up)
+    @pl.when(has_dn)
+    def _(): sig(dn)
+    pl.semaphore_wait(barrier,1+has_up.astype(jnp.int32)+has_dn.astype(jnp.int32))
+    def rc(src,dst,s,r,p):
+        return pltpu.make_async_remote_copy(src_ref=src,dst_ref=dst,send_sem=s,recv_sem=r,device_id={"dp":p},device_id_type=MESH)
+    def blk(j,zz): return outs[j].at[jnp.clip(zz,0,Z-1)*X+x]
+    locs=[]
+    for j in range(n):
+        c=pltpu.make_async_copy(ins[j],outs[j].at[me],loc.at[j]); c.start(); locs.append(c)
+    def send_up(j,s):
+        src = ins[j] if s==0 else blk(j,z-s)
+        return rc(src, outs[j].at[(jnp.maximum(z-s,0))*X+x], up_s.at[j,s], up_r.at[j,s], up)
+    def send_dn(j,s):
+        src = ins[j] if s==0 else blk(j,z+s)
+        return rc(src, outs[j].at[(jnp.minimum(z+s,Z-1))*X+x], dn_s.at[j,s], dn_r.at[j,s], dn)
+    def send_x(j,k,src,zz):
+        return rc(src, outs[j].at[zz*X+x], x_s.at[j,zz], x_r.at[j,zz], xp)
+    for s in range(Z):
+        for j in range(n):
+            if s>0:
+                @pl.when(z-s>=0)
+                def _():
+                    b=blk(j,z-s)
+                    pltpu.make_async_remote_copy(src_ref=b,dst_ref=b,send_sem=up_s.at[j,s-1],recv_sem=up_r.at[j,s-1],device_id={"dp":dn},device_id_type=MESH).wait_recv()
+                @pl.when(jnp.logical_and(z-s>=0,has_up))
+                def _(): send_up(j,s).start()
+                @pl.when(z-s>=0)
+                def _():
+                    zz=jnp.maximum(z-s,0); send_x(j,s,blk(j,z-s),zz).start()
+                @pl.when(z+s<Z)
+                def _():
+                    b=blk(j,z+s)
+                    pltpu.make_async_remote_copy(src_ref=b,dst_ref=b,send_sem=dn_s.at[j,s-1],recv_sem=dn_r.at[j,s-1],device_id={"dp":up},device_id_type=MESH).wait_recv()
+                @pl.when(jnp.logical_and(z+s<Z,has_dn))
+                def _(): send_dn(j,s).start()
+                @pl.when(z+s<Z)
+                def _():
+                    zz=jnp.minimum(z+s,Z-1); send_x(j,s,blk(j,z+s),zz).start()
+            else:
+                @pl.when(has_up)
+                def _(): send_up(j,0).start()
+                @pl.when(has_dn)
+                def _(): send_dn(j,0).start()
+                send_x(j,0,ins[j],z).start()
+    for j in range(n):
+        locs[j].wait()
+        for zz in range(Z):
+            b=outs[j].at[zz*X+(1-x)]
+            c=pltpu.make_async_remote_copy(src_ref=b,dst_ref=b,send_sem=x_s.at[j,zz],recv_sem=x_r.at[j,zz],device_id={"dp":xp},device_id_type=MESH)
+            c.wait_recv(); c.wait_send()
+        for s in range(Z-1):
+            @pl.when(jnp.logical_and(z-s>=0,has_up))
+            def _(): send_up(j,s).wait_send()
+            @pl.when(jnp.logical_and(z+s<Z,has_dn))
+            def _(): send_dn(j,s).wait_send()
+
+def gather(parts, dp, cid=1):
+    n=len(parts); Z=dp//2
+    sems=[pltpu.SemaphoreType.DMA((n,)),]+[pltpu.SemaphoreType.DMA((n,max(Z-1,1)))]*4+[pltpu.SemaphoreType.DMA((n,Z))]*2
+    return list(pl.pallas_call(functools.partial(gather_body,n),
+        out_shape=[jax.ShapeDtypeStruct((dp,)+p.shape,p.dtype) for p in parts],
+        in_specs=[pl.BlockSpec(memory_space=pltpu.VMEM)]*n,out_specs=[pl.BlockSpec(memory_space=pltpu.VMEM)]*n,
+        scratch_shapes=sems,
+        compiler_params=pltpu.CompilerParams(collective_id=cid,has_side_effects=True,vmem_limit_bytes=VMEM_LIMIT),name="gather%d"%n)(*parts))
+
+
 def layer_norm(activations, norm_gain, norm_shift):
     center = activations - jnp.mean(activations, -1, keepdims=True)
     inverse = lax.rsqrt(jnp.mean(center * center, -1, keepdims=True) + EPS)
@@ -257,30 +388,30 @@
     hidden_width = fc1_bias.shape[0]
     heads = width // HEAD_DIM
     _, slot_rows, model_width = images.shape
-    rows = up_to(slot_rows, 16)
+    rows = up_to(slot_rows, 32)
     columns = up_to(rows, LANES)
     kind = slot_kind[0]
 
-    block = jnp.concatenate(
+    small_vectors = jnp.stack(
+        (norm1_gain, norm1_shift, out_bias, gamma_attn, norm2_gain, norm2_shift, fc2_bias, gamma_mlp),
+        1,
+    )
+    first = jnp.concatenate(
         (
             qkv_weight.reshape(depth, 3 * width),
-            fc1_weight,
             out_weight.T,
-            fc2_weight.T,
+            jnp.pad(small_vectors, ((0, 0), (0, LANES - 8))),
         ),
         1,
     )
-    whole = lax.all_gather(block, "dp", axis=0, tiled=True)
+    first, fc1_matrix, fc2_turned = (
+        part.reshape(model_width, -1)
+        for part in gather((first, fc1_weight, fc2_weight.T), lax.axis_size("dp"))
+    )
     cuts = (3 * width, 3 * width + hidden_width, 4 * width + hidden_width)
-    qkv_matrix = whole[:, : cuts[0]]
-    fc1_matrix = whole[:, cuts[0] : cuts[1]]
-    out_turned = whole[:, cuts[1] : cuts[2]]
-    fc2_turned = whole[:, cuts[2] :]
-    small_vectors = jnp.stack(
-        (norm1_gain, norm1_shift, out_bias, gamma_attn, norm2_gain, norm2_shift, fc2_bias, gamma_mlp)
-    )
-    vectors = lax.all_gather(small_vectors, "dp", axis=0)
-    vectors = jnp.moveaxis(vectors, 0, 1).reshape(8, model_width).astype(f32)
+    qkv_matrix = first[:, : 3 * width]
+    out_turned = first[:, 3 * width : 4 * width]
+    vectors = first[:, 4 * width : 4 * width + 8].T.astype(f32)
 
     query_shift = query_bias.astype(f32)
     value_shift = value_bias.astype(f32)
@@ -308,14 +439,14 @@
     values = (projected[:, 2 * width :] + value_shift).astype(bf16)
     pieces = attend_forward(queries, keys, values, bias)
     branch_part = dot(pieces, out_turned, 1, 1)
-    branch = lax.psum(branch_part, "shard") + vectors[2]
+    branch = shard_sum(branch_part) + vectors[2]
     middle = inputs + vectors[3] * branch
     normed_two, normal_two, inverse_two = layer_norm(middle, vectors[4], vectors[5])
     normed_two = normed_two.astype(bf16)
     hidden = dot(normed_two, fc1_matrix, 1, 0) + hidden_shift
     active = jax.nn.gelu(hidden, approximate=False).astype(bf16)
     result_part = dot(active, fc2_turned, 1, 1)
-    result = lax.psum(result_part.astype(bf16), "shard").astype(f32) + vectors[6]
+    result = shard_sum(result_part) + vectors[6]
     layer_out = ((middle + vectors[7] * result) * live_rows).astype(bf16)[:slot_rows][None]
 
     grad_out = jnp.pad(out_grad[0], ((0, rows - slot_rows), (0, 0))).astype(f32) * live_rows
@@ -327,7 +458,7 @@
     grad_hidden = (grad_active * gelu_slope(hidden)).astype(bf16)
     grad_fc1_bias = jnp.sum(grad_hidden.astype(f32), 0)
     grad_fc1 = dot(normed_two, grad_hidden, 0, 0)
-    grad_normed_two = lax.psum(dot(grad_hidden, fc1_matrix, 1, 1), "shard")
+    grad_normed_two = shard_sum(dot(grad_hidden, fc1_matrix, 1, 1))
     grad_norm2_gain = jnp.sum(grad_normed_two * normal_two, 0)
     grad_norm2_shift = jnp.sum(grad_normed_two, 0)
     grad_middle = grad_out + norm_back(grad_normed_two, normal_two, inverse_two, vectors[4])
@@ -344,7 +475,7 @@
     grad_qkv = dot(normed_one, grad_projected, 0, 0)
     grad_query_bias = jnp.sum(grad_queries.astype(f32), 0)
     grad_value_bias = jnp.sum(grad_values.astype(f32), 0)
-    grad_normed_one = lax.psum(dot(grad_projected, qkv_matrix, 1, 1), "shard")
+    grad_normed_one = shard_sum(dot(grad_projected, qkv_matrix, 1, 1))
     grad_norm1_gain = jnp.sum(grad_normed_one * normal_one, 0)
     grad_norm1_shift = jnp.sum(grad_normed_one, 0)
     input_grad = grad_middle + norm_back(grad_normed_one, normal_one, inverse_one, vectors[0])

time: 456 us -> 374 us (0.82)
  waiting for transfers between devices: 167 us -> 0.01 us
  Pallas kernels: 73.2 us -> 199 us
  blocking collectives: 95.5 us -> 67.3 us
  between operations: 14.9 us -> 2.04 us
    psum x4 -> x0, waiting for transfers between devices: 160 us -> none  [the longest x1 45.1 us: on_device(): branch = lax.psum(branch_part, 'shard') + vectors[2]]
    pallas_call x0 -> x5, Pallas kernels: none -> 123 us  [the longest x4 74.2 us: shard_sum(): pl.pallas_call(functools.partial(shard_sum_body, chunks), out_shape=jax.S...]
    all_gather x1 -> x0, blocking collectives: 27.9 us -> none  [on_device(): vectors = lax.all_gather(small_vectors, 'dp', axis=0)]
    all_gather x1 -> x0, waiting for transfers between devices: 6.69 us -> none  [on_device(): whole = lax.all_gather(block, 'dp', axis=0, tiled=True)]
    unnamed x68 -> x71, local copies, waits for them, and re-layouts: 8.47 us -> 9.37 us
  transfers between devices with their start and end apart: 7 -> 2, of which waited for: 5 -> 0; matrix products, arithmetic and copies ran while one was open for 10% -> 7% of each run, Pallas kernels for 13% -> 9%
where the time goes in v2:
time: 374 us; the launch traced here: 368 us
  Pallas kernels  199 us (53%)
  blocking collectives  67.3 us (18%)
  local copies, waits for them, and re-layouts  31.4 us (8%)
  matrix products  30.2 us (8%)
  other arithmetic  27.8 us (7%)
  starting transfers between devices  11 us (3%)
    pallas_call x4, Pallas kernels, shard_sum(): pl.pallas_call(functools.partial(shard_sum_body, chunks), out_shape=jax.S...  74.2 us
    psum x1, blocking collectives, on_device(): lax.psum((small_sums, large_sums, grad_query_bias, grad_value_bias, grad_...  67.3 us
    pallas_call x1, Pallas kernels, gather(): pl.pallas_call(functools.partial(gather_body, n), out_shape=[jax.ShapeDty...  49.1 us
    pallas_call x1, Pallas kernels, table_sums(): pl.pallas_call(functools.partial(table_body, heads, groups), out_shape=ja...  34.9 us
    dot_general x12, matrix products, dot(): lax.dot_general(a, b, (((da,), (db,)), ((), ())), preferred_element_type=...  30.2 us
    pallas_call x1, Pallas kernels, gather_bias(): pl.pallas_call(functools.partial(bias_body, heads, groups), out_shape=jax...  25.9 us
    all_to_all x2, starting transfers between devices, sent_and_summed(): lax.all_to_all(parts, 'dp', split_axis=0, concat_axis=0, tiled=True)  11 us
    unnamed x71, local copies, waits for them, and re-layouts  9.37 us
  transfers between devices with their start and end apart: 2, of which 0 were waited for; matrix products, arithmetic and copies ran while one was open for 7% of the time, Pallas kernels for 9%

profile of v2, /device:TPU:0, one launch (start us, length us, event | category | flops | bytes accessed | tf_op | source)
XLA Modules:
  0.0 368.3 jit_solution(13581801473940905940)
XLA Ops:
  0.7 0.9 stack.62
  1.7 0.9 copy.95
  2.6 1.1 copy.94
  3.6 0.2 copy.97
  3.8 0.8 fusion.34.refs_0_
  4.5 49.1 %gather3.1 = (bf16[8,96,896]{2,1,0:T(8,128)(2,1)}, bf16[8,96,768]{2,1,0:T(8,128)(2,1)}, bf16[8,96,768]{2,1,0:T(8,128)(2,1)}) custom-call(bf16[96,896]{1,0:T(8,128)(2,1)} %fusion.34.refs_0_, bf16[96,768]{1,0:T(8,128)(2,1)} %refs_1_.1, bf16[96,768]{1,0:T(8,128)(2,1)} %bitcast.92), custom_call_target="tpu_custom_call" | custom-call | tf_op jit(solution)/shard_map/gather3/pallas_call | solution.py:315
  53.6 1.0 slice.125
  54.9 0.2 convert_reduce_fusion.1
  55.1 0.4 fusion.2
  55.5 1.1 fusion.28
  56.8 0.2 copy.113
  57.1 0.2 copy-done.22
  57.3 1.1 copy.111
  58.4 0.9 copy.112.k_ref
  59.3 1.8 tile.4
  61.0 3.1 tile.10
  64.8 0.6 reshape.182.table_ref
  65.5 2.8 select_select_fusion.index_ref
  68.3 25.9 %bias.1.bias_ref = bf16[3,608,640]{2,1,0:T(8,128)(2,1)} custom-call(s32[608,640]{1,0:T(8,128)} %select_select_fusion.index_ref, f32[54,128]{1,0:T(8,128)} %reshape.182.table_ref), custom_call_target="tpu_custom_call" | custom-call | flops 1000000000 | bytes 40000000 | tf_op jit(solution)/shard_map/bias/pallas_call | solution.py:70
  94.2 0.9 add_convert_fusion.2
  95.1 5.5 %attend_forward.1 = bf16[608,192]{1,0:T(8,128)(2,1)} custom-call(bf16[608,192]{1,0:T(8,128)(2,1)} %get-tuple-element.162.q_ref, bf16[608,192]{1,0:T(8,128)(2,1)} %copy.112.k_ref, bf16[608,192]{1,0:T(8,128)(2,1)} %get-tuple-element.161.v_ref, bf16[3,608,640]{2,1,0:T(8,128)(2,1)} %bias.1.bias_ref), custom_call_target="tpu_custom_call" | custom-call | flops 1000000000 | bytes 10000000 | tf_op jit(solution)/shard_map/attend_forward/pallas_call | solution.py:168
  100.6 3.0 fusion.31.part_ref
  103.6 18.5 %shard_sum4.4 = f32[608,768]{1,0:T(8,128)} custom-call(f32[608,768]{1,0:T(8,128)} %fusion.31.part_ref), custom_call_target="tpu_custom_call" | custom-call | tf_op jit(solution)/shard_map/shard_sum4/pallas_call | solution.py:236
  122.1 1.9 fusion.53
  124.0 0.4 multiply_reduce_fusion.6
  124.4 1.5 fusion.46
  125.9 6.2 %fusion.5 = (bf16[608,768]{1,0:T(8,128)(2,1)S(1)}, f32[608,768]{1,0:T(8,128)S(1)}) fusion(f32[768]{0:T(1024)S(1)} %convert_element_type.110, bf16[768,768]{1,0:T(8,128)(2,1)} %bitcast.107, f32[608,768]{1,0:T(8,128)S(1)} %get-tuple-element.138, f32[768]{0:T(1024)S(1)} %get-tuple-element.119, f32[768]{0:T(1024)S(1)} %get-tuple-element.120, ...), kind=kOutput, calls=%fused_computation.11 | convolution fusion | flops 750379008 | bytes 5863168 | tf_op jit(solution)/shard_map/dot_general | solution.py:38
  132.2 1.9 convert_reduce_fusion.2
  134.1 0.9 copy-done.26
  135.0 2.2 fusion.56.part_ref
  137.2 18.5 %shard_sum4.6 = f32[608,768]{1,0:T(8,128)} custom-call(f32[608,768]{1,0:T(8,128)} %fusion.56.part_ref), custom_call_target="tpu_custom_call" | custom-call | tf_op jit(solution)/shard_map/shard_sum4/pallas_call | solution.py:236
  155.8 2.4 multiply_reduce_fusion.1
  158.2 2.2 fusion.55.part_ref
  160.4 18.6 %shard_sum4.5 = f32[608,768]{1,0:T(8,128)} custom-call(f32[608,768]{1,0:T(8,128)} %fusion.55.part_ref), custom_call_target="tpu_custom_call" | custom-call | tf_op jit(solution)/shard_map/shard_sum4/pallas_call | solution.py:236
  179.0 3.6 multiply_reduce_fusion.2
  182.6 1.2 copy-done.2
  183.9 0.3 fusion.52
  184.1 0.9 copy-done.5
  185.1 1.8 convolution_convert_fusion.4
  186.8 0.9 copy.102.grad_ref
  187.7 9.0 %attend_backward.1 = (bf16[608,192]{1,0:T(8,128)(2,1)}, bf16[608,192]{1,0:T(8,128)(2,1)}, bf16[608,192]{1,0:T(8,128)(2,1)}, bf16[3,608,640]{2,1,0:T(8,128)(2,1)}) custom-call(bf16[608,192]{1,0:T(8,128)(2,1)} %get-tuple-element.162.q_ref, bf16[608,192]{1,0:T(8,128)(2,1)} %copy.112.k_ref, bf16[608,192]{1,0:T(8,128)(2,1)} %get-tuple-element.161.v_ref, ...), custom_call_target="tpu_custom_call" | custom-call | flops 2000000000 | bytes 20000000 | tf_op jit(solution)/shard_map/attend_backward/pallas_call | solution.py:182
  196.8 3.4 fusion.26.part_ref
  200.2 18.5 %shard_sum4.7 = f32[608,768]{1,0:T(8,128)} custom-call(f32[608,768]{1,0:T(8,128)} %fusion.26.part_ref), custom_call_target="tpu_custom_call" | custom-call | tf_op jit(solution)/shard_map/shard_sum4/pallas_call | solution.py:236
  218.7 4.0 %fusion.50 = (bf16[768]{0:T(1024)(128)(2,1)S(1)}, bf16[768]{0:T(1024)(128)(2,1)S(1)}, f32[608]{0:T(1024)S(1)}, f32[608]{0:T(1024)S(1)}, f32[608,768]{1,0:T(8,128)}, /*index=5*/f32[608,768]{1,0:T(8,128)}) fusion(f32[608,768]{1,0:T(8,128)} %shard_sum4.7, f32[608]{0:T(1024)S(1)} %add_rsqrt_fusion.1, f32[608]{0:T(1024)S(1)} %broadcast_multiply_fusion.6, ...), kind=kLoop, calls=%fused_computation.146 | loop fusion | flops 4666688 | bytes 6526976 | tf_op jit(solution)/shard_map/reduce_sum | solution.py:480
  223.4 0.6 copy.106
  224.1 5.0 %all-to-all-start.1 = ((bf16[8,96,8]{1,2,0:T(8,128)(2,1)}), bf16[8,96,8]{1,2,0:T(8,128)(2,1)S(1)}, u32[]{:S(2)}, u32[]{:S(2)}) async-start(bf16[8,96,8]{1,2,0:T(8,128)(2,1)} %copy.106), calls=%async_computation.1 | async-start | bytes 32768 | tf_op jit(solution)/shard_map/all_to_all | solution.py:493
  229.1 3.3 convolution_convert_fusion.2
  232.4 2.4 convolution_convert_fusion.1
  234.9 2.3 convolution_convert_fusion
  237.2 0.4 convolution_convert_fusion.3
  237.7 2.2 copy.103
  239.9 0.2 copy.109
  240.1 7.0 %concatenate.27 = bf16[8,96,2304]{2,1,0:T(8,128)(2,1)} concatenate(bf16[8,96,576]{2,1,0:T(8,128)(2,1)} %bitcast.76, bf16[8,96,768]{2,1,0:T(8,128)(2,1)} %bitcast.82, bf16[8,96,192]{2,1,0:T(8,128)(2,1)S(1)} %bitcast.81, bf16[8,96,768]{2,1,0:T(8,128)(2,1)} %bitcast.83), dimensions={2} | concatenate | bytes 7077888 | tf_op jit(solution)/shard_map/concatenate | solution.py:497
  247.0 6.0 %all-to-all-start = ((bf16[8,96,2304]{2,1,0:T(8,128)(2,1)}), bf16[8,96,2304]{2,1,0:T(8,128)(2,1)}, u32[]{:S(2)}, u32[]{:S(2)}) async-start(bf16[8,96,2304]{2,1,0:T(8,128)(2,1)} %concatenate.27), calls=%async_computation | async-start | bytes 7077888 | tf_op jit(solution)/shard_map/all_to_all | solution.py:493
  253.0 34.9 %table_sums.1 = f32[120,64]{1,0:T(8,128)} custom-call(s32[608,640]{1,0:T(8,128)} %select_select_fusion.index_ref, bf16[3,608,640]{2,1,0:T(8,128)(2,1)} %get-tuple-element.32.grad_ref), custom_call_target="tpu_custom_call" | custom-call | flops 2000000000 | bytes 60000000 | tf_op jit(solution)/shard_map/table_sums/pallas_call | solution.py:123
  288.0 0.9 reshape.180
  289.1 67.3 %all-reduce.7 = (f32[192]{0:T(256)}, f32[192]{0:T(256)}, f32[768]{0:T(1024)}, f32[732,3]{0,1:T(4,128)}, f32[2212,3]{0,1:T(4,128)}) all-reduce(f32[192]{0:T(256)S(1)} %convert_reduce_fusion.4, f32[192]{0:T(256)S(1)} %convert_reduce_fusion.3, f32[768]{0:T(1024)S(1)} %get-tuple-element.159, ...), channel_id=1, replica_groups=mesh['dp'=8,'shard'=4] {'dp'}, use_global_device_ids=true, to_apply=%region_19.20 | all-reduce | flops 9984 | bytes 79872 | tf_op jit(solution)/shard_map/psum | solution.py:486
  356.4 2.9 fusion.24
  359.3 2.9 fusion.25
  362.2 0.5 slice_bitcast_fusion.2
  362.7 2.6 convert_reduce_fusion
  365.4 0.9 slice_bitcast_fusion
  366.4 0.9 copy.107
  367.3 0.7 copy.108
  (99 shorter events, 1.8 us)
Async XLA Ops:
  0.7 54.2 %copy-start.4 = (bf16[1,591,768]{2,1,0:T(8,128)(2,1)S(1)}, bf16[1,591,768]{2,1,0:T(8,128)(2,1)}, u32[]{:S(2)}) copy-start(bf16[1,591,768]{2,1,0:T(8,128)(2,1)} %param.22) | copy-start | bytes 2723332
  53.6 1.9 copy-start.12
  56.7 0.7 copy-start.22
  56.7 1.7 copy-start.23
  56.8 2.5 copy-start.16
  61.0 3.8 %copy-start.17 = (bf16[2212,3]{0,1:T(4,128)(2,1)S(1)}, bf16[2212,3]{0,1:T(4,128)(2,1)}, u32[]{:S(2)}) copy-start(bf16[2212,3]{0,1:T(4,128)(2,1)} %param.43) | copy-start | bytes 39820
  61.0 3.8 %copy-start.18 = (bf16[732,3]{0,1:T(4,128)(2,1)S(1)}, bf16[732,3]{0,1:T(4,128)(2,1)}, u32[]{:S(2)}) copy-start(bf16[732,3]{0,1:T(4,128)(2,1)} %param.42) | copy-start | bytes 13180
  68.3 25.9 %copy-start.10 = (f32[608,192]{1,0:T(8,128)S(1)}, f32[608,192]{1,0:T(8,128)}, u32[]{:S(2)}) copy-start(f32[608,192]{1,0:T(8,128)} %copy.111) | copy-start | bytes 1400836
  103.6 18.5 %copy-start.19 = (bf16[768]{0:T(1024)(128)(2,1)S(1)}, bf16[768]{0:T(1024)(128)(2,1)}, u32[]{:S(2)}) copy-start(bf16[768]{0:T(1024)(128)(2,1)} %param.39) | copy-start | bytes 4612
  125.9 6.2 %copy-start.8 = (bf16[1,591,768]{2,1,0:T(8,128)(2,1)S(1)}, bf16[1,591,768]{2,1,0:T(8,128)(2,1)}, u32[]{:S(2)}) copy-start(bf16[1,591,768]{2,1,0:T(8,128)(2,1)} %param.23) | copy-start | bytes 2723332
  125.9 6.2 %copy-start.20 = (bf16[8,96,768]{2,1,0:T(8,128)(2,1)S(1)}, bf16[8,96,768]{2,1,0:T(8,128)(2,1)}, u32[]{:S(2)}) copy-start(bf16[8,96,768]{2,1,0:T(8,128)(2,1)} %get-tuple-element.28) | copy-start | bytes 3538948
  132.1 26.0 %copy-start.24 = (bf16[608,768]{1,0:T(8,128)(2,1)}, bf16[608,768]{1,0:T(8,128)(2,1)S(1)}, u32[]{:S(2)}) copy-start(bf16[608,768]{1,0:T(8,128)(2,1)S(1)} %get-tuple-element.157) | copy-start | bytes 2801668
  132.2 2.9 copy-start.21
  134.1 1.0 copy-start.26
  160.3 18.7 %copy-start = (f32[608,768]{1,0:T(8,128)S(1)}, f32[608,768]{1,0:T(8,128)}, u32[]{:S(2)}) copy-start(f32[608,768]{1,0:T(8,128)} %shard_sum4.4) | copy-start | bytes 5603332
  160.4 18.7 %copy-start.1 = (f32[608,768]{1,0:T(8,128)S(1)}, f32[608,768]{1,0:T(8,128)}, u32[]{:S(2)}) copy-start(f32[608,768]{1,0:T(8,128)} %shard_sum4.6) | copy-start | bytes 5603332
  182.6 1.2 copy-start.2
  184.1 1.0 copy-start.5
  187.7 9.0 %copy-start.13 = (bf16[8,96,896]{2,1,0:T(8,128)(2,1)S(1)}, bf16[8,96,896]{2,1,0:T(8,128)(2,1)}, u32[]{:S(2)}) copy-start(bf16[8,96,896]{2,1,0:T(8,128)(2,1)} %get-tuple-element.26) | copy-start | bytes 4128772
  218.7 10.4 %copy-start.14 = (bf16[608,192]{1,0:T(8,128)(2,1)S(1)}, bf16[608,192]{1,0:T(8,128)(2,1)}, u32[]{:S(2)}) copy-start(bf16[608,192]{1,0:T(8,128)(2,1)} %get-tuple-element.31) | copy-start | bytes 700420
  218.7 10.4 %copy-start.15 = (bf16[608,192]{1,0:T(8,128)(2,1)S(1)}, bf16[608,192]{1,0:T(8,128)(2,1)}, u32[]{:S(2)}) copy-start(bf16[608,192]{1,0:T(8,128)(2,1)} %get-tuple-element.29) | copy-start | bytes 700420
  224.1 23.0 %all-to-all-start.1 = ((bf16[8,96,8]{1,2,0:T(8,128)(2,1)}), bf16[8,96,8]{1,2,0:T(8,128)(2,1)S(1)}, u32[]{:S(2)}, u32[]{:S(2)}) async-start(bf16[8,96,8]{1,2,0:T(8,128)(2,1)} %copy.106), calls=%async_computation.1 | async-start | bytes 32768 | tf_op jit(solution)/shard_map/all_to_all | solution.py:493
  229.1 3.3 copy-start.27
  232.4 2.4 copy-start.9
  232.4 2.4 copy-start.25
  234.9 2.4 copy-start.6
  234.9 2.4 copy-start.11
  247.0 115.7 %all-to-all-start = ((bf16[8,96,2304]{2,1,0:T(8,128)(2,1)}), bf16[8,96,2304]{2,1,0:T(8,128)(2,1)}, u32[]{:S(2)}, u32[]{:S(2)}) async-start(bf16[8,96,2304]{2,1,0:T(8,128)(2,1)} %concatenate.27), calls=%async_computation | async-start | bytes 7077888 | tf_op jit(solution)/shard_map/all_to_all | solution.py:493
  356.4 2.9 copy-start.3
  356.4 2.9 copy-start.7
